TPU v7x, 256 devices: a whole 4x4x8 slice. The times are simulated.
256 devices in a mesh: gx: 32 (over x, y, core), gy: 8 (over z).
Axes of the slice: x: 4, y: 4, z: 8, core: 2. Of those that a mesh axis runs over, the one named last changes fastest.
Arguments:
- factor: bfloat16 [64, 256, 128, 256], P(None, 'gx', 'gy'), may hold values from -200 to 200
- offset: int32 [1], replicated, may hold values from 0 to 32
- diagonal: float32 [256, 128, 256], P('gx', 'gy'), may hold values from 0.25 to 16
- actuators: bfloat16 [8, 256, 128, 256], P(None, 'gx', 'gy'), may hold values from -200 to 200
- sensors: bfloat16 [8, 256, 128, 256], P(None, 'gx', 'gy'), may hold values from -200 to 200
Outputs:
- rotated: bfloat16 [32, 256, 128, 256], P(None, 'gx', 'gy')
- residual_factor: bfloat16 [32, 256, 128, 256], P(None, 'gx', 'gy')
- riccati: float32 [32, 32], replicated
- gram_first: float32 [32, 32], replicated
All inputs are finite; a program needn't handle non-finite values.
Results may differ from a plain program's by a relative error of at most 0.0034.
Values may be sent and summed in bfloat16 or wider, within the bound.
A program may use at most 128 MiB of HBM per device.

v0:
```python
import functools
import jax
import jax.numpy as jnp
from jax import lax
from jax.experimental import pallas as pl
from jax.experimental.pallas import tpu as pltpu
from jax.sharding import PartitionSpec as P

WINDOW = 32
KLEIN = 3
SMITH = 4
CONTROLS = 8
NX_LOC, NY_LOC, NZ = 8, 16, 256
CELLS = 256 * 128 * 256
MESH = pl.DeviceIdType.MESH
f32, bf16 = jnp.float32, jnp.bfloat16
HIGHEST = lax.Precision.HIGHEST


def dot(left, right, dims=((1,), (0,))):
    return lax.dot_general(left, right, (dims, ((), ())), precision=HIGHEST, preferred_element_type=f32)


def bdot(left, right, dims=((1,), (0,))):
    return lax.dot_general(left, right, (dims, ((), ())), preferred_element_type=f32)


def pieces(value, count):
    out = []
    rest = value
    for at in range(count):
        piece = rest.astype(bf16)
        out.append(piece)
        if at < count - 1:
            rest = rest - piece.astype(f32)
    return out


def peer_groups():
    gx = lax.axis_index("gx")
    z = lax.axis_index("gy")
    xy = gx // 2
    core = gx % 2
    return (
        (2, core, lambda d: (xy * 2 + (core + d) % 2, z)),
        (16, xy, lambda d: (((xy + d) % 16) * 2 + core, z)),
        (8, z, lambda d: (gx, (z + d) % 8)),
    )


def stats_kernel(w_hbm, diag_ref, as_ref, tot_ref, aw_hbm, wext, awbuf, acc, buf0, buf1, buf2,
                 in_sem, hs_sem, hr_sem, s_sem, r_sem, out_sem):
    gx = lax.axis_index("gx")
    gz = lax.axis_index("gy")
    bufs = (buf0, buf1, buf2)
    load = pltpu.make_async_copy(w_hbm, wext.at[pl.ds(1, NX_LOC), pl.ds(1, NY_LOC)], in_sem)
    load.start()
    barrier = pltpu.get_barrier_semaphore()
    right, left = ((gx + 1) % 32, gz), ((gx + 31) % 32, gz)
    up, down = (gx, (gz + 1) % 8), (gx, (gz + 7) % 8)
    count = 0
    for n, me, dev in peer_groups():
        for d in range(1, n):
            pl.semaphore_signal(barrier, inc=1, device_id=dev(d), device_id_type=MESH)
            count += 1
    for target in (right, left):
        pl.semaphore_signal(barrier, inc=1, device_id=target, device_id_type=MESH)
        count += 1
    load.wait()
    pl.semaphore_wait(barrier, count)
    inner_y = pl.ds(1, NY_LOC)
    inner_x = pl.ds(1, NX_LOC)
    moves = (
        (wext.at[NX_LOC, inner_y], wext.at[0, inner_y], right),
        (wext.at[1, inner_y], wext.at[NX_LOC + 1, inner_y], left),
        (wext.at[inner_x, NY_LOC], wext.at[inner_x, 0], up),
        (wext.at[inner_x, 1], wext.at[inner_x, NY_LOC + 1], down),
    )
    copies = []
    for at, (source, target, who) in enumerate(moves):
        copy = pltpu.make_async_remote_copy(source, target, hs_sem.at[at], hr_sem.at[at], device_id=who, device_id_type=MESH)
        copy.start()
        copies.append(copy)
    for copy in copies:
        copy.wait()

    @pl.when(gx == 0)
    def _():
        wext[0] = jnp.zeros_like(wext[0])

    @pl.when(gx == 31)
    def _():
        wext[NX_LOC + 1] = jnp.zeros_like(wext[0])

    @pl.when(gz == 0)
    def _():
        wext[:, 0] = jnp.zeros_like(wext[:, 0])

    @pl.when(gz == 7)
    def _():
        wext[:, NY_LOC + 1] = jnp.zeros_like(wext[:, 0])

    lane = lax.broadcasted_iota(jnp.int32, (WINDOW, NZ), 1)

    def line(at, total):
        x = at // NY_LOC
        y = at % NY_LOC
        w16 = wext[x + 1, y + 1]
        w = w16.astype(f32)
        beside = wext[x + 2, y + 1].astype(f32) + wext[x, y + 1].astype(f32)
        beside = beside + wext[x + 1, y + 2].astype(f32) + wext[x + 1, y].astype(f32)
        beside = beside + jnp.where(lane == NZ - 1, 0.0, pltpu.roll(w, NZ - 1, 1))
        beside = beside + jnp.where(lane == 0, 0.0, pltpu.roll(w, 1, 1))
        image = beside - (6.0 + diag_ref[x, pl.ds(y, 1), :]) * w
        parts = jnp.concatenate(pieces(image, 3), axis=0)
        awbuf[x, y] = parts
        stack = jnp.concatenate([w16, parts, as_ref[x, y]], axis=0)
        return total + bdot(stack, w16, ((1,), (1,)))

    def plane(x, total):
        return total + lax.fori_loop(0, NY_LOC, lambda y, t: line(x * NY_LOC + y, t), jnp.zeros((144, WINDOW), f32))

    total = lax.fori_loop(0, NX_LOC, plane, jnp.zeros((144, WINDOW), f32)) * (1.0 / CELLS)
    write = pltpu.make_async_copy(awbuf, aw_hbm, out_sem)
    write.start()
    gram = total[0:32]
    cross = (total[32:64] + (total[64:96] + total[96:128]))
    io = total[128:144]
    current = jnp.concatenate([
        jnp.concatenate([gram[8 * q:8 * q + 8] for q in range(4)], axis=1),
        jnp.concatenate([cross[8 * q:8 * q + 8] for q in range(4)], axis=1),
        jnp.concatenate([io[0:8], io[8:16], jnp.zeros((8, 64), f32)], axis=1),
    ], axis=0)
    for at, (n, me, dev) in enumerate(peer_groups()):
        buf = bufs[at]
        buf[me] = current
        for d in range(1, n):
            pltpu.make_async_remote_copy(buf.at[me], buf.at[me], s_sem.at[at], r_sem.at[at], device_id=dev(d), device_id_type=MESH).start()
        span = buf.at[pl.ds(0, n - 1)]
        pltpu.make_async_copy(span, span, r_sem.at[at]).wait()
        parts = [buf[j] for j in range(n)]
        while len(parts) > 1:
            parts = [parts[i] + parts[i + 1] for i in range(0, len(parts), 2)]
        current = parts[0]
    tot_ref[...] = current
    for at, (n, me, dev) in enumerate(peer_groups()):
        span = bufs[at].at[pl.ds(0, n - 1)]
        pltpu.make_async_copy(span, span, s_sem.at[at]).wait()
    write.wait()


def stats(w_t, diagonal, as_t):
    return pl.pallas_call(
        stats_kernel,
        out_shape=(jax.ShapeDtypeStruct((24, 128), f32), jax.ShapeDtypeStruct((NX_LOC, NY_LOC, 96, NZ), bf16)),
        in_specs=[pl.BlockSpec(memory_space=pl.ANY), pl.BlockSpec(memory_space=pltpu.VMEM), pl.BlockSpec(memory_space=pltpu.VMEM)],
        out_specs=(pl.BlockSpec(memory_space=pltpu.VMEM), pl.BlockSpec(memory_space=pl.ANY)),
        scratch_shapes=[
            pltpu.VMEM((NX_LOC + 2, NY_LOC + 2, WINDOW, NZ), bf16),
            pltpu.VMEM((NX_LOC, NY_LOC, 96, NZ), bf16),
            pltpu.VMEM((144, WINDOW), f32),
            pltpu.VMEM((2, 24, 128), f32), pltpu.VMEM((16, 24, 128), f32), pltpu.VMEM((8, 24, 128), f32),
            pltpu.SemaphoreType.DMA, pltpu.SemaphoreType.DMA((4,)), pltpu.SemaphoreType.DMA((4,)),
            pltpu.SemaphoreType.DMA((3,)), pltpu.SemaphoreType.DMA((3,)), pltpu.SemaphoreType.DMA,
        ],
        compiler_params=pltpu.CompilerParams(collective_id=0, has_side_effects=True, vmem_limit_bytes=40 << 20),
        name="stats_all_reduce",
    )(w_t, diagonal, as_t)


def eliminate(table, count):
    row_at = lax.broadcasted_iota(jnp.int32, table.shape, 0)
    for k in range(count):
        pivot_row = table[k:k + 1, :]
        factor = table[:, k:k + 1] * (1.0 / pivot_row[:, k:k + 1])
        table = jnp.where(row_at > k, table - factor * pivot_row, table)
    return table


def jordan(table, count):
    row_at = lax.broadcasted_iota(jnp.int32, table.shape, 0)
    for k in range(count):
        scaled = table[k:k + 1, :] * (1.0 / table[k:k + 1, k:k + 1])
        table = jnp.where(row_at == k, scaled, table - table[:, k:k + 1] * scaled)
    return table


def cholesky_rows(table):
    done = eliminate(table, WINDOW)
    row_at = lax.broadcasted_iota(jnp.int32, (WINDOW, WINDOW), 0)
    col_at = lax.broadcasted_iota(jnp.int32, (WINDOW, WINDOW), 1)
    pivots = jnp.sum(jnp.where(row_at == col_at, done[:, :WINDOW], 0.0), axis=1, keepdims=True)
    return done * (1.0 / jnp.sqrt(pivots))


def eye(n):
    return (lax.broadcasted_iota(jnp.int32, (n, n), 0) == lax.broadcasted_iota(jnp.int32, (n, n), 1)).astype(f32)


def small_algebra(totals):
    gram = jnp.concatenate([totals[0:8, 32 * q:32 * q + 32] for q in range(4)], axis=0)
    cross = jnp.concatenate([totals[8:16, 32 * q:32 * q + 32] for q in range(4)], axis=0)
    io_rows = jnp.concatenate([totals[16:24, 0:32], totals[16:24, 32:64]], axis=0)
    ident = eye(WINDOW)
    inverse_first = cholesky_rows(jnp.concatenate([gram, ident, jnp.zeros((WINDOW, 64), f32)], axis=1))[:, 32:64]
    both = dot(inverse_first, jnp.concatenate([gram, cross], axis=1))
    both = dot(jnp.concatenate([both[:, :32], both[:, 32:]], axis=0), inverse_first, ((1,), (1,)))
    gram_second, cross_first = both[:32], both[32:]
    io_first = dot(inverse_first, io_rows, ((1,), (1,)))
    second = cholesky_rows(jnp.concatenate([gram_second, ident, cross_first, io_first, jnp.zeros((WINDOW, 16), f32)], axis=1))
    inverse_second = second[:, 32:64]
    raw = dot(second[:, 64:96], inverse_second, ((1,), (1,)))
    projected = 0.5 * (raw + raw.T)
    drive = second[:, 96:104]
    sense = second[:, 104:112]
    transform = dot(inverse_second, inverse_first)
    shifted = jordan(jnp.concatenate([ident - projected, ident, jnp.zeros((WINDOW, 64), f32)], axis=1), WINDOW)
    inv_n = shifted[:, 32:64]
    inv_n_t = inv_n.T
    drive_t, sense_t = drive.T, sense.T
    hd_t = dot(drive_t, inv_n_t)
    riccati = None
    for iteration in range(KLEIN):
        if riccati is None:
            einv_t = -inv_n_t
            rows = sense_t
        else:
            q_t = dot(drive_t, riccati)
            hq_t = dot(q_t, inv_n_t)
            small = eye(CONTROLS) + dot(hd_t, q_t, ((1,), (1,)))
            small_t = small.T
            normal = dot(small_t, small)
            table = jnp.concatenate([normal, small_t, jnp.zeros((CONTROLS, 112), f32)], axis=1)
            small_inv = jordan(table, CONTROLS)[:, 8:16]
            middle = dot(small_inv, hd_t)
            einv_t = dot(middle, hq_t, ((0,), (0,))) - inv_n_t
            rows = jnp.concatenate([sense_t, q_t], axis=0)
        cayley_t = ident + 2.0 * einv_t
        chain = dot(rows, einv_t)
        for doubling in range(SMITH):
            chain = jnp.concatenate([chain, dot(chain, cayley_t)], axis=0)
            if doubling < SMITH - 1:
                cayley_t = dot(cayley_t, cayley_t)
        riccati = 2.0 * dot(chain, chain, ((0,), (0,)))
    rotate = dot(riccati, transform)
    remain = dot(dot(riccati, projected), transform)
    return rotate, remain, riccati, gram


def output_kernel(tot_ref, w_ref, aw_ref, rot_ref, res_ref, ric_ref, gram_ref, coef, tmp):
    @pl.when(pl.program_id(0) == 0)
    def _():
        rotate, remain, riccati, gram = small_algebra(tot_ref[...])
        ric_ref[...] = riccati
        gram_ref[...] = gram
        r0, r1, r2 = pieces(rotate, 3)
        m0, m1, m2 = pieces(-remain, 3)
        zero = jnp.zeros((WINDOW, 192), bf16)
        top = jnp.concatenate([r0, r1, r2, zero], axis=1)
        low = jnp.concatenate([m0, m1, m2, r0, r0, r0, r1, r1, r2], axis=1)
        coef[0:32, 0:288] = top
        coef[32:64, 0:288] = low

    def line(y, carry):
        w = w_ref[0, y]
        parts = aw_ref[0, y]
        hi, mid = parts[0:32], parts[32:64]
        data = jnp.concatenate([w, w, w, parts, hi, mid, hi], axis=0)
        tmp[y] = bdot(coef[:, 0:288], data)
        return carry

    lax.fori_loop(0, NY_LOC, line, 0)
    rot_ref[:, 0] = jnp.swapaxes(tmp[:, 0:32, :], 0, 1).astype(bf16)
    res_ref[:, 0] = jnp.swapaxes(tmp[:, 32:64, :], 0, 1).astype(bf16)


def outputs(totals, w_t, aw):
    field = (WINDOW, NX_LOC, NY_LOC, NZ)
    whole = lambda *shape: pl.BlockSpec(shape, lambda x: (0,) * len(shape))
    return pl.pallas_call(
        output_kernel,
        grid=(NX_LOC,),
        out_shape=(jax.ShapeDtypeStruct(field, bf16), jax.ShapeDtypeStruct(field, bf16),
                   jax.ShapeDtypeStruct((WINDOW, WINDOW), f32), jax.ShapeDtypeStruct((WINDOW, WINDOW), f32)),
        in_specs=[whole(24, 128),
                  pl.BlockSpec((1, NY_LOC, WINDOW, NZ), lambda x: (x, 0, 0, 0)),
                  pl.BlockSpec((1, NY_LOC, 96, NZ), lambda x: (x, 0, 0, 0))],
        out_specs=(pl.BlockSpec((WINDOW, 1, NY_LOC, NZ), lambda x: (0, x, 0, 0)),
                   pl.BlockSpec((WINDOW, 1, NY_LOC, NZ), lambda x: (0, x, 0, 0)),
                   whole(WINDOW, WINDOW), whole(WINDOW, WINDOW)),
        scratch_shapes=[pltpu.VMEM((64, 384), bf16), pltpu.VMEM((NY_LOC, 64, NZ), f32)],
        compiler_params=pltpu.CompilerParams(vmem_limit_bytes=40 << 20),
        name="algebra_outputs",
    )(totals, w_t, aw)


def local(factor, offset, diagonal, actuators, sensors):
    window = lax.dynamic_slice_in_dim(factor, offset[0], WINDOW, 0)
    w_t = jnp.transpose(window, (1, 2, 0, 3))
    as_t = jnp.transpose(jnp.concatenate([actuators, sensors], axis=0), (1, 2, 0, 3))
    totals, aw = stats(w_t, diagonal, as_t)
    rotated, residual, riccati, gram = outputs(totals, w_t, aw)
    return rotated, residual, riccati, gram


def solution(mesh):
    return jax.shard_map(
        local,
        mesh=mesh,
        in_specs=(P(None, "gx", "gy", None), P(), P("gx", "gy", None), P(None, "gx", "gy", None), P(None, "gx", "gy", None)),
        out_specs=(P(None, "gx", "gy", None), P(None, "gx", "gy", None), P(), P()),
        check_vma=False,
    )
```

profile of v0, /device:TPU:1, one launch (start us, length us, event | category | flops | bytes accessed | tf_op | source)
XLA Modules:
  0.0 103.2 jit_solution(780374636482264145)
XLA Ops:
  1.3 1.3 %copy.10 = bf16[8,8,16,256]{3,0,2,1:T(8,128)(2,1)S(1)} copy(bf16[8,8,16,256]{3,2,1,0:T(8,128)(2,1)} %param.8) | data formatting | bytes 1048576 | tf_op args[3]
  2.6 1.3 %copy.11 = bf16[8,8,16,256]{3,0,2,1:T(8,128)(2,1)S(1)} copy(bf16[8,8,16,256]{3,2,1,0:T(8,128)(2,1)} %param.9) | data formatting | bytes 1048576 | tf_op args[4]
  4.0 0.1 maximum_bitcast_fusion.as_ref
  4.0 1.8 %constant_dynamic-slice_fusion = bf16[32,8,16,256]{3,2,1,0:T(8,128)(2,1)S(1)} fusion(bf16[64,8,16,256]{3,2,1,0:T(8,128)(2,1)} %param.5, s32[]{:T(128)S(6)} %select_n.3), kind=kLoop, calls=%fused_computation.2 | loop fusion | bytes 4194308 | tf_op jit(solution)/shard_map/dynamic_slice | solution.py:298
  5.9 0.0 copy-start
  5.9 1.2 %copy.14 = bf16[32,8,16,256]{3,0,2,1:T(8,128)(2,1)S(1)} copy(bf16[32,8,16,256]{3,2,1,0:T(8,128)(2,1)S(1)} %constant_dynamic-slice_fusion) | data formatting | bytes 4194304
  7.0 0.0 copy-done
  7.1 56.3 %stats_all_reduce.1 = (f32[24,128]{1,0:T(8,128)S(1)}, bf16[8,16,96,256]{3,2,1,0:T(8,128)(2,1)S(1)}) custom-call(bf16[8,16,32,256]{3,2,1,0:T(8,128)(2,1)S(1)} %bitcast.9, f32[8,16,256]{2,1,0:T(8,128)S(1)} %copy-done, bf16[8,16,16,256]{3,2,1,0:T(8,128)(2,1)S(1)} %maximum_bitcast_fusion.as_ref), custom_call_target="tpu_custom_call" | custom-call | tf_op jit(solution)/shard_map/stats_all_reduce/pallas_call | solution.py:153
  63.4 39.8 %algebra_outputs.1 = (bf16[32,8,16,256]{3,2,1,0:T(8,128)(2,1)}, bf16[32,8,16,256]{3,2,1,0:T(8,128)(2,1)}, f32[32,32]{1,0:T(8,128)}, f32[32,32]{1,0:T(8,128)}) custom-call(f32[24,128]{1,0:T(8,128)S(1)} %get-tuple-element.6.tot_ref, bf16[8,16,32,256]{3,2,1,0:T(8,128)(2,1)S(1)} %bitcast.10, bf16[8,16,96,256]{3,2,1,0:T(8,128)(2,1)S(1)} %get-tuple-element.7.aw_ref), custom_call_target="tpu_custom_call" | custom-call | tf_op jit(solution)/shard_map/algebra_outputs/pallas_call | solution.py:280
Async XLA Ops:
  5.9 1.2 %copy-start = (f32[8,16,256]{2,1,0:T(8,128)S(1)}, f32[8,16,256]{2,1,0:T(8,128)}, u32[]{:S(2)}) copy-start(f32[8,16,256]{2,1,0:T(8,128)} %diag_ref.1) | copy-start | bytes 393220
where the time goes:
time: 103 us
  Pallas kernels  96.1 us (93%)
  local copies, waits for them, and re-layouts  5.66 us (5%)
  between operations  1.33 us (1%)
    pallas_call x1, Pallas kernels, stats(): pl.pallas_call(stats_kernel, out_shape=(jax.ShapeDtypeStruct((24, 128), f...  56.3 us
    pallas_call x1, Pallas kernels, outputs(): pl.pallas_call(output_kernel, grid=(NX_LOC,), out_shape=(jax.ShapeDtypeSt...  39.8 us
    unnamed x5, local copies, waits for them, and re-layouts  3.85 us

commit v1 on v0

v1 whole, which is shorter than its diff:
```python
import functools
import jax
import jax.numpy as jnp
from jax import lax
from jax.experimental import pallas as pl
from jax.experimental.pallas import tpu as pltpu
from jax.sharding import PartitionSpec as P

WINDOW = 32
KLEIN = 3
SMITH = 4
CONTROLS = 8
NX_LOC, NY_LOC, NZ = 8, 16, 256
CELLS = 256 * 128 * 256
MESH = pl.DeviceIdType.MESH
f32, bf16 = jnp.float32, jnp.bfloat16
HIGHEST = lax.Precision.HIGHEST


def dot(left, right, dims=((1,), (0,))):
    return lax.dot_general(left, right, (dims, ((), ())), precision=HIGHEST, preferred_element_type=f32)


def bdot(left, right, dims=((1,), (0,))):
    return lax.dot_general(left, right, (dims, ((), ())), preferred_element_type=f32)


def pieces(value, count):
    out = []
    rest = value
    for at in range(count):
        piece = rest.astype(bf16)
        out.append(piece)
        if at < count - 1:
            rest = rest - piece.astype(f32)
    return out


def peer_groups():
    gx = lax.axis_index("gx")
    z = lax.axis_index("gy")
    xy = gx // 2
    core = gx % 2
    return (
        (2, core, lambda d: (xy * 2 + (core + d) % 2, z)),
        (16, xy, lambda d: (((xy + d) % 16) * 2 + core, z)),
        (8, z, lambda d: (gx, (z + d) % 8)),
    )


def tree_sum(parts):
    while len(parts) > 1:
        parts = [parts[i] + parts[i + 1] for i in range(0, len(parts) - 1, 2)] + parts[len(parts) - len(parts) % 2:]
    return parts[0]


class Reduction:
    def __init__(self, bufs, s_sem, r_sem):
        self.bufs, self.s_sem, self.r_sem = bufs, s_sem, r_sem
        self.groups = peer_groups()

    def send(self, at, value):
        n, me, dev = self.groups[at]
        buf = self.bufs[at]
        buf[me] = value
        for d in range(1, n):
            pltpu.make_async_remote_copy(buf.at[me], buf.at[me], self.s_sem.at[at], self.r_sem.at[at],
                                         device_id=dev(d), device_id_type=MESH).start()

    def receive(self, at):
        n = self.groups[at][0]
        buf = self.bufs[at]
        span = buf.at[pl.ds(0, n - 1)]
        pltpu.make_async_copy(span, span, self.r_sem.at[at]).wait()
        return tree_sum([buf[j] for j in range(n)])

    def finish(self):
        for at, (n, me, dev) in enumerate(self.groups):
            span = self.bufs[at].at[pl.ds(0, n - 1)]
            pltpu.make_async_copy(span, span, self.s_sem.at[at]).wait()


def fold(rows):
    return jnp.concatenate([rows[8 * q:8 * q + 8] for q in range(4)], axis=1)


def unfold(block):
    return jnp.concatenate([block[:, 32 * q:32 * q + 32] for q in range(4)], axis=0)


def stats_kernel(off_ref, fac_hbm, diag_ref, act_hbm, sen_hbm, small_ref, w_hbm, aw_hbm,
                 fac, io, wext, io_t, awbuf, g0, g1, g2, s0, s1, s2,
                 in_sem, hs_sem, hr_sem, gs_sem, gr_sem, ss_sem, sr_sem, out_sem):
    gx = lax.axis_index("gx")
    gz = lax.axis_index("gy")
    loads = [pltpu.make_async_copy(fac_hbm, fac, in_sem.at[0]),
             pltpu.make_async_copy(act_hbm, io.at[pl.ds(0, CONTROLS)], in_sem.at[1]),
             pltpu.make_async_copy(sen_hbm, io.at[pl.ds(CONTROLS, CONTROLS)], in_sem.at[2])]
    for load in loads:
        load.start()
    barrier = pltpu.get_barrier_semaphore()
    right, left = ((gx + 1) % 32, gz), ((gx + 31) % 32, gz)
    up, down = (gx, (gz + 1) % 8), (gx, (gz + 7) % 8)
    count = 0
    for n, me, dev in peer_groups():
        for d in range(1, n):
            pl.semaphore_signal(barrier, inc=1, device_id=dev(d), device_id_type=MESH)
            count += 1
    for target in (right, left):
        pl.semaphore_signal(barrier, inc=1, device_id=target, device_id_type=MESH)
        count += 1
    start = off_ref[0]
    loads[0].wait()

    def turn(x, total):
        plane = fac[pl.ds(start, WINDOW), x].astype(f32)
        wext[x + 1, pl.ds(1, NY_LOC)] = jnp.swapaxes(plane, 0, 1).astype(bf16)
        part = jnp.zeros((WINDOW, WINDOW), f32)
        for y in range(NY_LOC):
            rows = wext[x + 1, y + 1]
            part = part + bdot(rows, rows, ((1,), (1,)))
        return total + part

    gram_local = lax.fori_loop(0, NX_LOC, turn, jnp.zeros((WINDOW, WINDOW), f32)) * (1.0 / CELLS)
    pl.semaphore_wait(barrier, count)
    inner_y = pl.ds(1, NY_LOC)
    inner_x = pl.ds(1, NX_LOC)
    moves = (
        (wext.at[NX_LOC, inner_y], wext.at[0, inner_y], right),
        (wext.at[1, inner_y], wext.at[NX_LOC + 1, inner_y], left),
        (wext.at[inner_x, NY_LOC], wext.at[inner_x, 0], up),
        (wext.at[inner_x, 1], wext.at[inner_x, NY_LOC + 1], down),
    )
    copies = []
    for at, (source, target, who) in enumerate(moves):
        copy = pltpu.make_async_remote_copy(source, target, hs_sem.at[at], hr_sem.at[at], device_id=who, device_id_type=MESH)
        copy.start()
        copies.append(copy)
    gram_sum = Reduction((g0, g1, g2), gs_sem, gr_sem)
    cross_sum = Reduction((s0, s1, s2), ss_sem, sr_sem)
    gram_sum.send(0, fold(gram_local))
    w_write = pltpu.make_async_copy(wext.at[inner_x, inner_y], w_hbm, out_sem.at[0])
    w_write.start()
    loads[1].wait()
    loads[2].wait()

    def turn_io(x, carry):
        io_t[x] = jnp.swapaxes(io[:, x].astype(f32), 0, 1).astype(bf16)
        return carry

    lax.fori_loop(0, NX_LOC, turn_io, 0)
    gram_sum.send(1, gram_sum.receive(0))

    lane = lax.broadcasted_iota(jnp.int32, (WINDOW, NZ), 1)

    def line(x, y):
        w16 = wext[x + 1, y + 1]
        w = w16.astype(f32)
        beside = wext[x + 2, y + 1].astype(f32) + wext[x, y + 1].astype(f32)
        beside = beside + wext[x + 1, y + 2].astype(f32) + wext[x + 1, y].astype(f32)
        beside = beside + jnp.where(lane == NZ - 1, 0.0, pltpu.roll(w, NZ - 1, 1))
        beside = beside + jnp.where(lane == 0, 0.0, pltpu.roll(w, 1, 1))
        image = beside - (6.0 + diag_ref[x, y:y + 1, :]) * w
        parts = jnp.concatenate(pieces(image, 3), axis=0)
        awbuf[x, y] = parts
        return bdot(jnp.concatenate([parts, io_t[x, y]], axis=0), w16, ((1,), (1,)))

    def lines(ys):
        def body(x, total):
            part = jnp.zeros((112, WINDOW), f32)
            for y in ys:
                part = part + line(x, y)
            return total + part
        return body

    total = lax.fori_loop(1, NX_LOC - 1, lines(range(1, NY_LOC - 1)), jnp.zeros((112, WINDOW), f32))
    for copy in copies:
        copy.wait()
    w_write.wait()

    @pl.when(gx == 0)
    def _():
        wext[0] = jnp.zeros_like(wext[0])

    @pl.when(gx == 31)
    def _():
        wext[NX_LOC + 1] = jnp.zeros_like(wext[0])

    @pl.when(gz == 0)
    def _():
        wext[:, 0] = jnp.zeros_like(wext[:, 0])

    @pl.when(gz == 7)
    def _():
        wext[:, NY_LOC + 1] = jnp.zeros_like(wext[:, 0])

    def edge(step, total):
        return lines((0, NY_LOC - 1))(2 * step + 2, lines((0, NY_LOC - 1))(2 * step + 1, total))

    total = lax.fori_loop(0, (NX_LOC - 2) // 2, edge, total)
    total = lax.fori_loop(0, 2, lambda at, t: lines(range(NY_LOC))(at * (NX_LOC - 1), t), total)
    total = total * (1.0 / CELLS)
    cross = total[0:32] + (total[32:64] + total[64:96])
    io_sum = jnp.concatenate([total[96:104], total[104:112], jnp.zeros((8, 64), f32)], axis=1)
    cross_sum.send(0, jnp.concatenate([fold(cross), io_sum], axis=0))
    aw_write = pltpu.make_async_copy(awbuf, aw_hbm, out_sem.at[1])
    aw_write.start()
    gram_sum.send(2, gram_sum.receive(1))
    cross_sum.send(1, cross_sum.receive(0))
    gram = unfold(gram_sum.receive(2))
    ident = eye(WINDOW)
    table = jnp.concatenate([gram, ident, jnp.zeros((WINDOW, 64), f32)], axis=1)
    table = eliminate(table, 0, 16)
    cross_sum.send(2, cross_sum.receive(1))
    inverse_first = unit_pivots(eliminate(table, 16, WINDOW))[:, 32:64]
    gram_second = dot(dot(inverse_first, gram), inverse_first, ((1,), (1,)))
    table = jnp.concatenate([gram_second, ident, jnp.zeros((WINDOW, 64), f32)], axis=1)
    inverse_second = unit_pivots(eliminate(table, 0, WINDOW))[:, 32:64]
    transform = dot(inverse_second, inverse_first)
    received = cross_sum.receive(2)
    cross = unfold(received[0:8])
    io_rows = jnp.concatenate([received[8:16, 0:32], received[8:16, 32:64]], axis=0)
    raw = dot(dot(transform, cross), transform, ((1,), (1,)))
    io_basis = dot(transform, io_rows, ((1,), (1,)))
    small_ref[0:32] = jnp.concatenate([raw, transform, io_basis, jnp.zeros((WINDOW, 48), f32)], axis=1)
    small_ref[32:64] = jnp.concatenate([gram, jnp.zeros((WINDOW, 96), f32)], axis=1)
    gram_sum.finish()
    cross_sum.finish()
    aw_write.wait()


def stats(offset, factor, diagonal, actuators, sensors):
    vmem, anywhere = pl.BlockSpec(memory_space=pltpu.VMEM), pl.BlockSpec(memory_space=pl.ANY)
    dma = pltpu.SemaphoreType.DMA
    return pl.pallas_call(
        stats_kernel,
        out_shape=(jax.ShapeDtypeStruct((64, 128), f32),
                   jax.ShapeDtypeStruct((NX_LOC, NY_LOC, WINDOW, NZ), bf16),
                   jax.ShapeDtypeStruct((NX_LOC, NY_LOC, 96, NZ), bf16)),
        in_specs=[pl.BlockSpec(memory_space=pltpu.SMEM), anywhere, vmem, anywhere, anywhere],
        out_specs=(vmem, anywhere, anywhere),
        scratch_shapes=[
            pltpu.VMEM((64, NX_LOC, NY_LOC, NZ), bf16),
            pltpu.VMEM((2 * CONTROLS, NX_LOC, NY_LOC, NZ), bf16),
            pltpu.VMEM((NX_LOC + 2, NY_LOC + 2, WINDOW, NZ), bf16),
            pltpu.VMEM((NX_LOC, NY_LOC, 2 * CONTROLS, NZ), bf16),
            pltpu.VMEM((NX_LOC, NY_LOC, 96, NZ), bf16),
            pltpu.VMEM((2, 8, 128), f32), pltpu.VMEM((16, 8, 128), f32), pltpu.VMEM((8, 8, 128), f32),
            pltpu.VMEM((2, 16, 128), f32), pltpu.VMEM((16, 16, 128), f32), pltpu.VMEM((8, 16, 128), f32),
            dma((3,)), dma((4,)), dma((4,)), dma((3,)), dma((3,)), dma((3,)), dma((3,)), dma((2,)),
        ],
        compiler_params=pltpu.CompilerParams(collective_id=0, has_side_effects=True, vmem_limit_bytes=40 << 20),
        name="stats_all_reduce",
    )(offset, factor, diagonal, actuators, sensors)


def eliminate(table, first, last):
    row_at = lax.broadcasted_iota(jnp.int32, table.shape, 0)
    for k in range(first, last):
        pivot_row = table[k:k + 1, :]
        factor = table[:, k:k + 1] * (1.0 / pivot_row[:, k:k + 1])
        table = jnp.where(row_at > k, table - factor * pivot_row, table)
    return table


def jordan(table, count):
    row_at = lax.broadcasted_iota(jnp.int32, table.shape, 0)
    for k in range(count):
        scaled = table[k:k + 1, :] * (1.0 / table[k:k + 1, k:k + 1])
        table = jnp.where(row_at == k, scaled, table - table[:, k:k + 1] * scaled)
    return table


def unit_pivots(done):
    row_at = lax.broadcasted_iota(jnp.int32, (WINDOW, WINDOW), 0)
    col_at = lax.broadcasted_iota(jnp.int32, (WINDOW, WINDOW), 1)
    pivots = jnp.sum(jnp.where(row_at == col_at, done[:, :WINDOW], 0.0), axis=1, keepdims=True)
    return done * (1.0 / jnp.sqrt(pivots))


def eye(n):
    return (lax.broadcasted_iota(jnp.int32, (n, n), 0) == lax.broadcasted_iota(jnp.int32, (n, n), 1)).astype(f32)


def small_algebra(small):
    ident = eye(WINDOW)
    raw = small[0:32, 0:32]
    transform = small[0:32, 32:64]
    projected = 0.5 * (raw + raw.T)
    drive = small[0:32, 64:72]
    sense = small[0:32, 72:80]
    gram = small[32:64, 0:32]
    shifted = jordan(jnp.concatenate([ident - projected, ident, jnp.zeros((WINDOW, 64), f32)], axis=1), WINDOW)
    inv_n = shifted[:, 32:64]
    inv_n_t = inv_n.T
    drive_t, sense_t = drive.T, sense.T
    hd_t = dot(drive_t, inv_n_t)
    riccati = None
    for iteration in range(KLEIN):
        if riccati is None:
            einv_t = -inv_n_t
            rows = sense_t
        else:
            q_t = dot(drive_t, riccati)
            hq_t = dot(q_t, inv_n_t)
            small = eye(CONTROLS) + dot(hd_t, q_t, ((1,), (1,)))
            small_t = small.T
            normal = dot(small_t, small)
            table = jnp.concatenate([normal, small_t, jnp.zeros((CONTROLS, 112), f32)], axis=1)
            small_inv = jordan(table, CONTROLS)[:, 8:16]
            middle = dot(small_inv, hd_t)
            einv_t = dot(middle, hq_t, ((0,), (0,))) - inv_n_t
            rows = jnp.concatenate([sense_t, q_t], axis=0)
        cayley_t = ident + 2.0 * einv_t
        chain = dot(rows, einv_t)
        for doubling in range(SMITH):
            chain = jnp.concatenate([chain, dot(chain, cayley_t)], axis=0)
            if doubling < SMITH - 1:
                cayley_t = dot(cayley_t, cayley_t)
        riccati = 2.0 * dot(chain, chain, ((0,), (0,)))
    rotate = dot(riccati, transform)
    remain = dot(dot(riccati, projected), transform)
    return rotate, remain, riccati, gram


def output_kernel(tot_ref, w_ref, aw_ref, rot_ref, res_ref, ric_ref, gram_ref, coef, tmp):
    @pl.when(pl.program_id(0) == 0)
    def _():
        rotate, remain, riccati, gram = small_algebra(tot_ref[...])
        ric_ref[...] = riccati
        gram_ref[...] = gram
        r0, r1, r2 = pieces(rotate, 3)
        m0, m1, m2 = pieces(-remain, 3)
        zero = jnp.zeros((WINDOW, WINDOW), bf16)
        cat = lambda *blocks: jnp.concatenate(blocks, axis=1)
        coef[...] = jnp.concatenate([
            cat(r0, zero, zero, zero), cat(m0, r0, r0, r0),
            cat(r1, zero, zero, zero), cat(m1, r1, r1, zero),
            cat(r2, zero, zero, zero), cat(m2, r2, zero, zero)], axis=0)

    for y in range(NY_LOC):
        data = jnp.concatenate([w_ref[0, y], aw_ref[0, y]], axis=0)
        out = bdot(coef[...], data)
        tmp[y] = out[0:64] + (out[64:128] + out[128:192])
    rot_ref[:, 0] = jnp.swapaxes(tmp[:, 0:32, :], 0, 1).astype(bf16)
    res_ref[:, 0] = jnp.swapaxes(tmp[:, 32:64, :], 0, 1).astype(bf16)


def outputs(totals, w_t, aw):
    field = (WINDOW, NX_LOC, NY_LOC, NZ)
    whole = lambda *shape: pl.BlockSpec(shape, lambda x: (0,) * len(shape))
    return pl.pallas_call(
        output_kernel,
        grid=(NX_LOC,),
        out_shape=(jax.ShapeDtypeStruct(field, bf16), jax.ShapeDtypeStruct(field, bf16),
                   jax.ShapeDtypeStruct((WINDOW, WINDOW), f32), jax.ShapeDtypeStruct((WINDOW, WINDOW), f32)),
        in_specs=[whole(64, 128),
                  pl.BlockSpec((1, NY_LOC, WINDOW, NZ), lambda x: (x, 0, 0, 0)),
                  pl.BlockSpec((1, NY_LOC, 96, NZ), lambda x: (x, 0, 0, 0))],
        out_specs=(pl.BlockSpec((WINDOW, 1, NY_LOC, NZ), lambda x: (0, x, 0, 0)),
                   pl.BlockSpec((WINDOW, 1, NY_LOC, NZ), lambda x: (0, x, 0, 0)),
                   whole(WINDOW, WINDOW), whole(WINDOW, WINDOW)),
        scratch_shapes=[pltpu.VMEM((192, 128), bf16), pltpu.VMEM((NY_LOC, 64, NZ), f32)],
        compiler_params=pltpu.CompilerParams(vmem_limit_bytes=40 << 20),
        name="algebra_outputs",
    )(totals, w_t, aw)


def local(factor, offset, diagonal, actuators, sensors):
    small, w_t, aw = stats(offset, factor, diagonal, actuators, sensors)
    return outputs(small, w_t, aw)


def solution(mesh):
    return jax.shard_map(
        local,
        mesh=mesh,
        in_specs=(P(None, "gx", "gy", None), P(), P("gx", "gy", None), P(None, "gx", "gy", None), P(None, "gx", "gy", None)),
        out_specs=(P(None, "gx", "gy", None), P(None, "gx", "gy", None), P(), P()),
        check_vma=False,
    )
```

time: 103 us -> 56.9 us (0.55)
  Pallas kernels: 96.1 us -> 50.1 us
    pallas_call x1, Pallas kernels: 39.8 us -> 15.9 us  [outputs(): pl.pallas_call(output_kernel, grid=(NX_LOC,), out_shape=(jax.ShapeDtypeSt...]
    pallas_call x1, Pallas kernels: 56.3 us -> 34.1 us  [stats(): pl.pallas_call(stats_kernel, out_shape=(jax.ShapeDtypeStruct((64, 128), f...]
    dynamic_slice x1 -> x0, local copies, waits for them, and re-layouts: 1.8 us -> none  [local(): window = lax.dynamic_slice_in_dim(factor, offset[0], WINDOW, 0)]
    unnamed x5 -> x8, local copies, waits for them, and re-layouts: 3.85 us -> 5.17 us
where the time goes in v1:
time: 56.9 us; the launch traced here: 56.5 us
  Pallas kernels  50.1 us (88%)
  local copies, waits for them, and re-layouts  5.17 us (9%)
  between operations  1.3 us (2%)
    pallas_call x1, Pallas kernels, stats(): pl.pallas_call(stats_kernel, out_shape=(jax.ShapeDtypeStruct((64, 128), f...  34.1 us
    pallas_call x1, Pallas kernels, outputs(): pl.pallas_call(output_kernel, grid=(NX_LOC,), out_shape=(jax.ShapeDtypeSt...  15.9 us
    unnamed x8, local copies, waits for them, and re-layouts  5.17 us

profile of v1, /device:TPU:1, one launch (start us, length us, event | category | flops | bytes accessed | tf_op | source)
XLA Modules:
  0.0 56.5 jit_solution(9873394776667048750)
XLA Ops:
  1.3 0.0 copy-start
  1.3 2.2 %copy-done = bf16[64,8,16,256]{3,2,1,0:T(8,128)(2,1)S(1)} copy-done((bf16[64,8,16,256]{3,2,1,0:T(8,128)(2,1)S(1)}, bf16[64,8,16,256]{3,2,1,0:T(8,128)(2,1)}, u32[]{:S(2)}) %copy-start) | copy-done | bytes 4194328
  3.5 0.0 copy-start.1
  3.5 1.0 %copy-done.1 = bf16[8,8,16,256]{3,2,1,0:T(8,128)(2,1)S(1)} copy-done((bf16[8,8,16,256]{3,2,1,0:T(8,128)(2,1)S(1)}, bf16[8,8,16,256]{3,2,1,0:T(8,128)(2,1)}, u32[]{:S(2)}) %copy-start.1) | copy-done | bytes 524312
  4.5 0.0 copy-start.2
  4.5 1.0 %copy-done.2 = bf16[8,8,16,256]{3,2,1,0:T(8,128)(2,1)S(1)} copy-done((bf16[8,8,16,256]{3,2,1,0:T(8,128)(2,1)S(1)}, bf16[8,8,16,256]{3,2,1,0:T(8,128)(2,1)}, u32[]{:S(2)}) %copy-start.2) | copy-done | bytes 524312
  5.5 0.0 copy-start.3
  5.6 0.9 %copy-done.3 = f32[8,16,256]{2,1,0:T(8,128)S(1)} copy-done((f32[8,16,256]{2,1,0:T(8,128)S(1)}, f32[8,16,256]{2,1,0:T(8,128)}, u32[]{:S(2)}) %copy-start.3) | copy-done | bytes 131096
  6.5 34.1 %stats_all_reduce.1 = (f32[64,128]{1,0:T(8,128)S(1)}, bf16[8,16,32,256]{3,2,1,0:T(8,128)(2,1)S(1)}, bf16[8,16,96,256]{3,2,1,0:T(8,128)(2,1)S(1)}) custom-call(s32[1]{0:T(128)S(6)} %copy.9.off_ref, bf16[64,8,16,256]{3,2,1,0:T(8,128)(2,1)S(1)} %copy-done, f32[8,16,256]{2,1,0:T(8,128)S(1)} %copy-done.3, bf16[8,8,16,256]{3,2,1,0:T(8,128)(2,1)S(1)} %copy-done.1, ...), custom_call_target="tpu_custom_call" | custom-call | tf_op jit(solution)/shard_map/stats_all_reduce/pallas_call | solution.py:235
  40.6 15.9 %algebra_outputs.1 = (bf16[32,8,16,256]{3,2,1,0:T(8,128)(2,1)}, bf16[32,8,16,256]{3,2,1,0:T(8,128)(2,1)}, f32[32,32]{1,0:T(8,128)}, f32[32,32]{1,0:T(8,128)}) custom-call(f32[64,128]{1,0:T(8,128)S(1)} %get-tuple-element.7.tot_ref, bf16[8,16,32,256]{3,2,1,0:T(8,128)(2,1)S(1)} %get-tuple-element.8.w_ref, bf16[8,16,96,256]{3,2,1,0:T(8,128)(2,1)S(1)} %get-tuple-element.9.aw_ref), custom_call_target="tpu_custom_call" | custom-call | tf_op jit(solution)/shard_map/algebra_outputs/pallas_call | solution.py:352
Async XLA Ops:
  1.3 2.2 %copy-start = (bf16[64,8,16,256]{3,2,1,0:T(8,128)(2,1)S(1)}, bf16[64,8,16,256]{3,2,1,0:T(8,128)(2,1)}, u32[]{:S(2)}) copy-start(bf16[64,8,16,256]{3,2,1,0:T(8,128)(2,1)} %fac_hbm.1) | copy-start | bytes 12582916
  3.5 1.0 %copy-start.1 = (bf16[8,8,16,256]{3,2,1,0:T(8,128)(2,1)S(1)}, bf16[8,8,16,256]{3,2,1,0:T(8,128)(2,1)}, u32[]{:S(2)}) copy-start(bf16[8,8,16,256]{3,2,1,0:T(8,128)(2,1)} %act_hbm.1) | copy-start | bytes 1572868
  4.5 1.0 %copy-start.2 = (bf16[8,8,16,256]{3,2,1,0:T(8,128)(2,1)S(1)}, bf16[8,8,16,256]{3,2,1,0:T(8,128)(2,1)}, u32[]{:S(2)}) copy-start(bf16[8,8,16,256]{3,2,1,0:T(8,128)(2,1)} %sen_hbm.1) | copy-start | bytes 1572868
  5.5 0.9 %copy-start.3 = (f32[8,16,256]{2,1,0:T(8,128)S(1)}, f32[8,16,256]{2,1,0:T(8,128)}, u32[]{:S(2)}) copy-start(f32[8,16,256]{2,1,0:T(8,128)} %diag_ref.1) | copy-start | bytes 393220

commit v2 on v1

--- a/solution.py
+++ b/solution.py
@@ -23,6 +23,12 @@
 
 def bdot(left, right, dims=((1,), (0,))):
     return lax.dot_general(left, right, (dims, ((), ())), preferred_element_type=f32)
+
+
+def dot3(left, right, dims=((1,), (0,))):
+    left_hi, left_lo = pieces(left, 2)
+    right_hi, right_lo = pieces(right, 2)
+    return bdot(left_hi, right_hi, dims) + (bdot(left_hi, right_lo, dims) + bdot(left_lo, right_hi, dims))
 
 
 def pieces(value, count):
@@ -88,14 +94,15 @@
     return jnp.concatenate([block[:, 32 * q:32 * q + 32] for q in range(4)], axis=0)
 
 
-def stats_kernel(off_ref, fac_hbm, diag_ref, act_hbm, sen_hbm, small_ref, w_hbm, aw_hbm,
-                 fac, io, wext, io_t, awbuf, g0, g1, g2, s0, s1, s2,
+def stats_kernel(off_ref, fac_hbm, diag_hbm, act_hbm, sen_hbm, small_ref, w_hbm, aw_hbm,
+                 fac, diag_ref, io, wext, io_t, awbuf, g0, g1, g2, s0, s1, s2,
                  in_sem, hs_sem, hr_sem, gs_sem, gr_sem, ss_sem, sr_sem, out_sem):
     gx = lax.axis_index("gx")
     gz = lax.axis_index("gy")
     loads = [pltpu.make_async_copy(fac_hbm, fac, in_sem.at[0]),
              pltpu.make_async_copy(act_hbm, io.at[pl.ds(0, CONTROLS)], in_sem.at[1]),
-             pltpu.make_async_copy(sen_hbm, io.at[pl.ds(CONTROLS, CONTROLS)], in_sem.at[2])]
+             pltpu.make_async_copy(sen_hbm, io.at[pl.ds(CONTROLS, CONTROLS)], in_sem.at[2]),
+             pltpu.make_async_copy(diag_hbm, diag_ref, in_sem.at[3])]
     for load in loads:
         load.start()
     barrier = pltpu.get_barrier_semaphore()
@@ -112,16 +119,12 @@
     start = off_ref[0]
     loads[0].wait()
 
-    def turn(x, total):
+    def turn(x, carry):
         plane = fac[pl.ds(start, WINDOW), x].astype(f32)
         wext[x + 1, pl.ds(1, NY_LOC)] = jnp.swapaxes(plane, 0, 1).astype(bf16)
-        part = jnp.zeros((WINDOW, WINDOW), f32)
-        for y in range(NY_LOC):
-            rows = wext[x + 1, y + 1]
-            part = part + bdot(rows, rows, ((1,), (1,)))
-        return total + part
-
-    gram_local = lax.fori_loop(0, NX_LOC, turn, jnp.zeros((WINDOW, WINDOW), f32)) * (1.0 / CELLS)
+        return carry
+
+    lax.fori_loop(0, NX_LOC, turn, 0)
     pl.semaphore_wait(barrier, count)
     inner_y = pl.ds(1, NY_LOC)
     inner_x = pl.ds(1, NX_LOC)
@@ -136,13 +139,22 @@
         copy = pltpu.make_async_remote_copy(source, target, hs_sem.at[at], hr_sem.at[at], device_id=who, device_id_type=MESH)
         copy.start()
         copies.append(copy)
+
+    def gram_plane(x, total):
+        part = jnp.zeros((WINDOW, WINDOW), f32)
+        for y in range(NY_LOC):
+            rows = wext[x + 1, y + 1]
+            part = part + bdot(rows, rows, ((1,), (1,)))
+        return total + part
+
+    gram_local = lax.fori_loop(0, NX_LOC, gram_plane, jnp.zeros((WINDOW, WINDOW), f32)) * (1.0 / CELLS)
     gram_sum = Reduction((g0, g1, g2), gs_sem, gr_sem)
     cross_sum = Reduction((s0, s1, s2), ss_sem, sr_sem)
     gram_sum.send(0, fold(gram_local))
     w_write = pltpu.make_async_copy(wext.at[inner_x, inner_y], w_hbm, out_sem.at[0])
     w_write.start()
-    loads[1].wait()
-    loads[2].wait()
+    for load in loads[1:]:
+        load.wait()
 
     def turn_io(x, carry):
         io_t[x] = jnp.swapaxes(io[:, x].astype(f32), 0, 1).astype(bf16)
@@ -207,15 +219,14 @@
     aw_write.start()
     gram_sum.send(2, gram_sum.receive(1))
     cross_sum.send(1, cross_sum.receive(0))
+    cross_sum.send(2, cross_sum.receive(1))
     gram = unfold(gram_sum.receive(2))
     ident = eye(WINDOW)
     table = jnp.concatenate([gram, ident, jnp.zeros((WINDOW, 64), f32)], axis=1)
-    table = eliminate(table, 0, 16)
-    cross_sum.send(2, cross_sum.receive(1))
-    inverse_first = unit_pivots(eliminate(table, 16, WINDOW))[:, 32:64]
+    inverse_first = unit_pivots(sweep(table, WINDOW, False))[:, 32:64]
     gram_second = dot(dot(inverse_first, gram), inverse_first, ((1,), (1,)))
     table = jnp.concatenate([gram_second, ident, jnp.zeros((WINDOW, 64), f32)], axis=1)
-    inverse_second = unit_pivots(eliminate(table, 0, WINDOW))[:, 32:64]
+    inverse_second = unit_pivots(sweep(table, WINDOW, False))[:, 32:64]
     transform = dot(inverse_second, inverse_first)
     received = cross_sum.receive(2)
     cross = unfold(received[0:8])
@@ -230,44 +241,54 @@
 
 
 def stats(offset, factor, diagonal, actuators, sensors):
-    vmem, anywhere = pl.BlockSpec(memory_space=pltpu.VMEM), pl.BlockSpec(memory_space=pl.ANY)
+    vmem, anywhere = pl.BlockSpec(memory_space=pltpu.VMEM), pl.BlockSpec(memory_space=pltpu.HBM)
     dma = pltpu.SemaphoreType.DMA
     return pl.pallas_call(
         stats_kernel,
         out_shape=(jax.ShapeDtypeStruct((64, 128), f32),
                    jax.ShapeDtypeStruct((NX_LOC, NY_LOC, WINDOW, NZ), bf16),
                    jax.ShapeDtypeStruct((NX_LOC, NY_LOC, 96, NZ), bf16)),
-        in_specs=[pl.BlockSpec(memory_space=pltpu.SMEM), anywhere, vmem, anywhere, anywhere],
+        in_specs=[pl.BlockSpec(memory_space=pltpu.SMEM), anywhere, anywhere, anywhere, anywhere],
         out_specs=(vmem, anywhere, anywhere),
         scratch_shapes=[
             pltpu.VMEM((64, NX_LOC, NY_LOC, NZ), bf16),
+            pltpu.VMEM((NX_LOC, NY_LOC, NZ), f32),
             pltpu.VMEM((2 * CONTROLS, NX_LOC, NY_LOC, NZ), bf16),
             pltpu.VMEM((NX_LOC + 2, NY_LOC + 2, WINDOW, NZ), bf16),
             pltpu.VMEM((NX_LOC, NY_LOC, 2 * CONTROLS, NZ), bf16),
             pltpu.VMEM((NX_LOC, NY_LOC, 96, NZ), bf16),
             pltpu.VMEM((2, 8, 128), f32), pltpu.VMEM((16, 8, 128), f32), pltpu.VMEM((8, 8, 128), f32),
             pltpu.VMEM((2, 16, 128), f32), pltpu.VMEM((16, 16, 128), f32), pltpu.VMEM((8, 16, 128), f32),
-            dma((3,)), dma((4,)), dma((4,)), dma((3,)), dma((3,)), dma((3,)), dma((3,)), dma((2,)),
+            dma((4,)), dma((4,)), dma((4,)), dma((3,)), dma((3,)), dma((3,)), dma((3,)), dma((2,)),
         ],
-        compiler_params=pltpu.CompilerParams(collective_id=0, has_side_effects=True, vmem_limit_bytes=40 << 20),
+        compiler_params=pltpu.CompilerParams(collective_id=0, has_side_effects=True, vmem_limit_bytes=60 << 20),
         name="stats_all_reduce",
     )(offset, factor, diagonal, actuators, sensors)
 
 
-def eliminate(table, first, last):
+def sweep(table, count, upward):
     row_at = lax.broadcasted_iota(jnp.int32, table.shape, 0)
-    for k in range(first, last):
-        pivot_row = table[k:k + 1, :]
-        factor = table[:, k:k + 1] * (1.0 / pivot_row[:, k:k + 1])
-        table = jnp.where(row_at > k, table - factor * pivot_row, table)
-    return table
-
-
-def jordan(table, count):
-    row_at = lax.broadcasted_iota(jnp.int32, table.shape, 0)
-    for k in range(count):
-        scaled = table[k:k + 1, :] * (1.0 / table[k:k + 1, k:k + 1])
-        table = jnp.where(row_at == k, scaled, table - table[:, k:k + 1] * scaled)
+    for start in range(0, count, 8):
+        columns = [jnp.broadcast_to(table[:, k:k + 1], table.shape) for k in range(start, start + 8)]
+        for at in range(0, 8, 2):
+            k = start + at
+            col0, col1 = columns[at], columns[at + 1]
+            a, b, c, d = col0[k:k + 1], col1[k:k + 1], col0[k + 1:k + 2], col1[k + 1:k + 2]
+            inverse = 1.0 / (a * d - b * c)
+
+            def step(value):
+                row0, row1 = value[k:k + 1], value[k + 1:k + 2]
+                scaled0 = (row0 * d - row1 * b) * inverse
+                scaled1 = (row1 * a - row0 * c) * inverse
+                other = value - (col0 * scaled0 + col1 * scaled1)
+                if upward:
+                    return jnp.where(row_at == k, scaled0, jnp.where(row_at == k + 1, scaled1, other))
+                inner = row1 - row0 * (c / a)
+                return jnp.where(row_at > k + 1, other, jnp.where(row_at == k + 1, inner, value))
+
+            table = step(table)
+            for later in range(at + 2, 8):
+                columns[later] = step(columns[later])
     return table
 
 
@@ -290,80 +311,90 @@
     drive = small[0:32, 64:72]
     sense = small[0:32, 72:80]
     gram = small[32:64, 0:32]
-    shifted = jordan(jnp.concatenate([ident - projected, ident, jnp.zeros((WINDOW, 64), f32)], axis=1), WINDOW)
+    shifted = sweep(jnp.concatenate([ident - projected, ident, jnp.zeros((WINDOW, 64), f32)], axis=1), WINDOW, True)
     inv_n = shifted[:, 32:64]
-    inv_n_t = inv_n.T
     drive_t, sense_t = drive.T, sense.T
-    hd_t = dot(drive_t, inv_n_t)
-    riccati = None
+    hd = dot3(inv_n, drive)
+    hd_t = hd.T
+    chain = None
     for iteration in range(KLEIN):
-        if riccati is None:
-            einv_t = -inv_n_t
+        if chain is None:
+            einv_t = -inv_n
             rows = sense_t
         else:
-            q_t = dot(drive_t, riccati)
-            hq_t = dot(q_t, inv_n_t)
-            small = eye(CONTROLS) + dot(hd_t, q_t, ((1,), (1,)))
-            small_t = small.T
-            normal = dot(small_t, small)
-            table = jnp.concatenate([normal, small_t, jnp.zeros((CONTROLS, 112), f32)], axis=1)
-            small_inv = jordan(table, CONTROLS)[:, 8:16]
-            middle = dot(small_inv, hd_t)
-            einv_t = dot(middle, hq_t, ((0,), (0,))) - inv_n_t
+            q_t = 2.0 * dot3(dot3(drive_t, chain, ((1,), (1,))), chain)
+            hq_t = dot3(q_t, inv_n)
+            small = eye(CONTROLS) + dot3(hd_t, q_t, ((1,), (1,)))
+            normal = dot3(small, small, ((1,), (1,)))
+            table = jnp.concatenate([normal, dot3(small, hq_t), jnp.zeros((CONTROLS, 88), f32)], axis=1)
+            solved = sweep(table, CONTROLS, True)[:, CONTROLS:CONTROLS + WINDOW]
+            einv_t = dot3(hd, solved) - inv_n
             rows = jnp.concatenate([sense_t, q_t], axis=0)
         cayley_t = ident + 2.0 * einv_t
-        chain = dot(rows, einv_t)
+        chain = dot3(rows, einv_t)
         for doubling in range(SMITH):
-            chain = jnp.concatenate([chain, dot(chain, cayley_t)], axis=0)
+            chain = jnp.concatenate([chain, dot3(chain, cayley_t)], axis=0)
             if doubling < SMITH - 1:
-                cayley_t = dot(cayley_t, cayley_t)
-        riccati = 2.0 * dot(chain, chain, ((0,), (0,)))
+                cayley_t = dot3(cayley_t, cayley_t)
+    riccati = 2.0 * dot3(chain, chain, ((0,), (0,)))
     rotate = dot(riccati, transform)
     remain = dot(dot(riccati, projected), transform)
     return rotate, remain, riccati, gram
 
 
-def output_kernel(tot_ref, w_ref, aw_ref, rot_ref, res_ref, ric_ref, gram_ref, coef, tmp):
-    @pl.when(pl.program_id(0) == 0)
-    def _():
-        rotate, remain, riccati, gram = small_algebra(tot_ref[...])
-        ric_ref[...] = riccati
-        gram_ref[...] = gram
-        r0, r1, r2 = pieces(rotate, 3)
-        m0, m1, m2 = pieces(-remain, 3)
-        zero = jnp.zeros((WINDOW, WINDOW), bf16)
-        cat = lambda *blocks: jnp.concatenate(blocks, axis=1)
-        coef[...] = jnp.concatenate([
-            cat(r0, zero, zero, zero), cat(m0, r0, r0, r0),
-            cat(r1, zero, zero, zero), cat(m1, r1, r1, zero),
-            cat(r2, zero, zero, zero), cat(m2, r2, zero, zero)], axis=0)
-
-    for y in range(NY_LOC):
-        data = jnp.concatenate([w_ref[0, y], aw_ref[0, y]], axis=0)
-        out = bdot(coef[...], data)
-        tmp[y] = out[0:64] + (out[64:128] + out[128:192])
-    rot_ref[:, 0] = jnp.swapaxes(tmp[:, 0:32, :], 0, 1).astype(bf16)
-    res_ref[:, 0] = jnp.swapaxes(tmp[:, 32:64, :], 0, 1).astype(bf16)
-
-
-def outputs(totals, w_t, aw):
+def output_kernel(small_ref, w_hbm, aw_hbm, rot_hbm, res_hbm, ric_ref, gram_ref,
+                  wbuf, awbuf, rot, res, coef, tmp, in_sem, out_sem):
+    loads = [pltpu.make_async_copy(w_hbm, wbuf, in_sem.at[0]), pltpu.make_async_copy(aw_hbm, awbuf, in_sem.at[1])]
+    for load in loads:
+        load.start()
+    rotate, remain, riccati, gram = small_algebra(small_ref[...])
+    ric_ref[...] = riccati
+    gram_ref[...] = gram
+    r0, r1, r2 = pieces(rotate, 3)
+    m0, m1, m2 = pieces(-remain, 3)
+    zero = jnp.zeros((WINDOW, WINDOW), bf16)
+    cat = lambda *blocks: jnp.concatenate(blocks, axis=1)
+    coef[...] = jnp.concatenate([
+        cat(r0, zero, zero, zero), cat(m0, r0, r0, r0),
+        cat(r1, zero, zero, zero), cat(m1, r1, r1, zero),
+        cat(r2, zero, zero, zero), cat(m2, r2, zero, zero)], axis=0)
+    for load in loads:
+        load.wait()
+
+    def plane(x, carry):
+        for y in range(NY_LOC):
+            data = jnp.concatenate([wbuf[x, y], awbuf[x, y]], axis=0)
+            out = bdot(coef[...], data)
+            tmp[y] = out[0:64] + (out[64:128] + out[128:192])
+        rot[x] = jnp.swapaxes(tmp[:, 0:32, :], 0, 1).astype(bf16)
+        res[x] = jnp.swapaxes(tmp[:, 32:64, :], 0, 1).astype(bf16)
+        pltpu.make_async_copy(rot.at[x], rot_hbm.at[:, x], out_sem.at[0]).start()
+        pltpu.make_async_copy(res.at[x], res_hbm.at[:, x], out_sem.at[1]).start()
+        return carry
+
+    lax.fori_loop(0, NX_LOC, plane, 0)
+    pltpu.make_async_copy(rot, rot, out_sem.at[0]).wait()
+    pltpu.make_async_copy(res, res, out_sem.at[1]).wait()
+
+
+def outputs(small, w_t, aw):
     field = (WINDOW, NX_LOC, NY_LOC, NZ)
-    whole = lambda *shape: pl.BlockSpec(shape, lambda x: (0,) * len(shape))
+    vmem, hbm = pl.BlockSpec(memory_space=pltpu.VMEM), pl.BlockSpec(memory_space=pltpu.HBM)
     return pl.pallas_call(
         output_kernel,
-        grid=(NX_LOC,),
         out_shape=(jax.ShapeDtypeStruct(field, bf16), jax.ShapeDtypeStruct(field, bf16),
                    jax.ShapeDtypeStruct((WINDOW, WINDOW), f32), jax.ShapeDtypeStruct((WINDOW, WINDOW), f32)),
-        in_specs=[whole(64, 128),
-                  pl.BlockSpec((1, NY_LOC, WINDOW, NZ), lambda x: (x, 0, 0, 0)),
-                  pl.BlockSpec((1, NY_LOC, 96, NZ), lambda x: (x, 0, 0, 0))],
-        out_specs=(pl.BlockSpec((WINDOW, 1, NY_LOC, NZ), lambda x: (0, x, 0, 0)),
-                   pl.BlockSpec((WINDOW, 1, NY_LOC, NZ), lambda x: (0, x, 0, 0)),
-                   whole(WINDOW, WINDOW), whole(WINDOW, WINDOW)),
-        scratch_shapes=[pltpu.VMEM((192, 128), bf16), pltpu.VMEM((NY_LOC, 64, NZ), f32)],
-        compiler_params=pltpu.CompilerParams(vmem_limit_bytes=40 << 20),
+        in_specs=[vmem, hbm, hbm],
+        out_specs=(hbm, hbm, vmem, vmem),
+        scratch_shapes=[
+            pltpu.VMEM((NX_LOC, NY_LOC, WINDOW, NZ), bf16), pltpu.VMEM((NX_LOC, NY_LOC, 96, NZ), bf16),
+            pltpu.VMEM((NX_LOC, WINDOW, NY_LOC, NZ), bf16), pltpu.VMEM((NX_LOC, WINDOW, NY_LOC, NZ), bf16),
+            pltpu.VMEM((192, 128), bf16), pltpu.VMEM((NY_LOC, 64, NZ), f32),
+            pltpu.SemaphoreType.DMA((2,)), pltpu.SemaphoreType.DMA((2,)),
+        ],
+        compiler_params=pltpu.CompilerParams(vmem_limit_bytes=60 << 20),
         name="algebra_outputs",
-    )(totals, w_t, aw)
+    )(small, w_t, aw)
 
 
 def local(factor, offset, diagonal, actuators, sensors):

time: 56.9 us -> 44.5 us (0.78)
  Pallas kernels: 50.1 us -> 42.5 us
  local copies, waits for them, and re-layouts: 5.17 us -> 0 us
    unnamed x8 -> x0, local copies, waits for them, and re-layouts: 5.17 us -> none
    pallas_call x1, Pallas kernels: 34.1 us -> 29.8 us  [stats(): pl.pallas_call(stats_kernel, out_shape=(jax.ShapeDtypeStruct((64, 128), f...]
    pallas_call x1, Pallas kernels: 15.9 us -> 12.7 us  [outputs(): pl.pallas_call(output_kernel, out_shape=(jax.ShapeDtypeStruct(field, bf16...]
where the time goes in v2:
time: 44.5 us; the launch traced here: 43.8 us
  Pallas kernels  42.5 us (96%)
  between operations  1.28 us (3%)
    pallas_call x1, Pallas kernels, stats(): pl.pallas_call(stats_kernel, out_shape=(jax.ShapeDtypeStruct((64, 128), f...  29.8 us
    pallas_call x1, Pallas kernels, outputs(): pl.pallas_call(output_kernel, out_shape=(jax.ShapeDtypeStruct(field, bf16...  12.7 us

profile of v2, /device:TPU:1, one launch (start us, length us, event | category | flops | bytes accessed | tf_op | source)
XLA Modules:
  0.0 43.8 jit_solution(5862357388754945679)
XLA Ops:
  1.3 29.8 %stats_all_reduce.1 = (f32[64,128]{1,0:T(8,128)}, bf16[8,16,32,256]{3,2,1,0:T(8,128)(2,1)}, bf16[8,16,96,256]{3,2,1,0:T(8,128)(2,1)}) custom-call(s32[1]{0:T(128)S(6)} %copy.9.off_ref, bf16[64,8,16,256]{3,2,1,0:T(8,128)(2,1)} %fac_hbm.1, f32[8,16,256]{2,1,0:T(8,128)} %diag_hbm.1, bf16[8,8,16,256]{3,2,1,0:T(8,128)(2,1)} %act_hbm.1, ...), custom_call_target="tpu_custom_call" | custom-call | tf_op jit(solution)/shard_map/stats_all_reduce/pallas_call | solution.py:246
  31.1 12.7 %algebra_outputs.1 = (bf16[32,8,16,256]{3,2,1,0:T(8,128)(2,1)}, bf16[32,8,16,256]{3,2,1,0:T(8,128)(2,1)}, f32[32,32]{1,0:T(8,128)}, f32[32,32]{1,0:T(8,128)}) custom-call(f32[64,128]{1,0:T(8,128)} %get-tuple-element.7.small_ref, bf16[8,16,32,256]{3,2,1,0:T(8,128)(2,1)} %get-tuple-element.8.w_hbm, bf16[8,16,96,256]{3,2,1,0:T(8,128)(2,1)} %get-tuple-element.9.aw_hbm), custom_call_target="tpu_custom_call" | custom-call | tf_op jit(solution)/shard_map/algebra_outputs/pallas_call | solution.py:383

commit v3 on v2

--- a/solution.py
+++ b/solution.py
@@ -47,10 +47,13 @@
     z = lax.axis_index("gy")
     xy = gx // 2
     core = gx % 2
+    x, y = xy // 4, xy % 4
+    plane = sorted(((dx, dy) for dx in range(4) for dy in range(4) if dx or dy),
+                   key=lambda d: -(min(d[0], 4 - d[0]) + min(d[1], 4 - d[1])))
     return (
-        (2, core, lambda d: (xy * 2 + (core + d) % 2, z)),
-        (16, xy, lambda d: (((xy + d) % 16) * 2 + core, z)),
-        (8, z, lambda d: (gx, (z + d) % 8)),
+        (2, core, [(xy * 2 + (core + 1) % 2, z)]),
+        (16, xy, [((((x + dx) % 4) * 4 + (y + dy) % 4) * 2 + core, z) for dx, dy in plane]),
+        (8, z, [(gx, (z + dz) % 8) for dz in (4, 3, 5, 2, 6, 1, 7)]),
     )
 
 
@@ -66,12 +69,12 @@
         self.groups = peer_groups()
 
     def send(self, at, value):
-        n, me, dev = self.groups[at]
+        n, me, peers = self.groups[at]
         buf = self.bufs[at]
         buf[me] = value
-        for d in range(1, n):
+        for peer in peers:
             pltpu.make_async_remote_copy(buf.at[me], buf.at[me], self.s_sem.at[at], self.r_sem.at[at],
-                                         device_id=dev(d), device_id_type=MESH).start()
+                                         device_id=peer, device_id_type=MESH).start()
 
     def receive(self, at):
         n = self.groups[at][0]
@@ -81,7 +84,7 @@
         return tree_sum([buf[j] for j in range(n)])
 
     def finish(self):
-        for at, (n, me, dev) in enumerate(self.groups):
+        for at, (n, me, peers) in enumerate(self.groups):
             span = self.bufs[at].at[pl.ds(0, n - 1)]
             pltpu.make_async_copy(span, span, self.s_sem.at[at]).wait()
 
@@ -95,50 +98,67 @@
 
 
 def stats_kernel(off_ref, fac_hbm, diag_hbm, act_hbm, sen_hbm, small_ref, w_hbm, aw_hbm,
-                 fac, diag_ref, io, wext, io_t, awbuf, g0, g1, g2, s0, s1, s2,
+                 fac_ends, fac_mid, diag_ref, io, wext, xhalo, yhalo, io_t, awbuf, g0, g1, g2, s0, s1, s2,
                  in_sem, hs_sem, hr_sem, gs_sem, gr_sem, ss_sem, sr_sem, out_sem):
     gx = lax.axis_index("gx")
     gz = lax.axis_index("gy")
-    loads = [pltpu.make_async_copy(fac_hbm, fac, in_sem.at[0]),
-             pltpu.make_async_copy(act_hbm, io.at[pl.ds(0, CONTROLS)], in_sem.at[1]),
-             pltpu.make_async_copy(sen_hbm, io.at[pl.ds(CONTROLS, CONTROLS)], in_sem.at[2]),
-             pltpu.make_async_copy(diag_hbm, diag_ref, in_sem.at[3])]
+    last = NX_LOC - 1
+    loads = [pltpu.make_async_copy(fac_hbm.at[:, 0], fac_ends.at[0], in_sem.at[0]),
+             pltpu.make_async_copy(fac_hbm.at[:, last], fac_ends.at[1], in_sem.at[1]),
+             pltpu.make_async_copy(fac_hbm.at[:, pl.ds(1, NX_LOC - 2)], fac_mid, in_sem.at[2]),
+             pltpu.make_async_copy(act_hbm, io.at[pl.ds(0, CONTROLS)], in_sem.at[3]),
+             pltpu.make_async_copy(sen_hbm, io.at[pl.ds(CONTROLS, CONTROLS)], in_sem.at[4]),
+             pltpu.make_async_copy(diag_hbm, diag_ref, in_sem.at[5])]
     for load in loads:
         load.start()
     barrier = pltpu.get_barrier_semaphore()
     right, left = ((gx + 1) % 32, gz), ((gx + 31) % 32, gz)
     up, down = (gx, (gz + 1) % 8), (gx, (gz + 7) % 8)
     count = 0
-    for n, me, dev in peer_groups():
-        for d in range(1, n):
-            pl.semaphore_signal(barrier, inc=1, device_id=dev(d), device_id_type=MESH)
+    for n, me, peers in peer_groups():
+        for peer in peers:
+            pl.semaphore_signal(barrier, inc=1, device_id=peer, device_id_type=MESH)
             count += 1
     for target in (right, left):
         pl.semaphore_signal(barrier, inc=1, device_id=target, device_id_type=MESH)
         count += 1
     start = off_ref[0]
-    loads[0].wait()
-
-    def turn(x, carry):
-        plane = fac[pl.ds(start, WINDOW), x].astype(f32)
-        wext[x + 1, pl.ds(1, NY_LOC)] = jnp.swapaxes(plane, 0, 1).astype(bf16)
-        return carry
-
-    lax.fori_loop(0, NX_LOC, turn, 0)
-    pl.semaphore_wait(barrier, count)
     inner_y = pl.ds(1, NY_LOC)
     inner_x = pl.ds(1, NX_LOC)
+    side_x = jnp.zeros((NY_LOC + 2, WINDOW, NZ), bf16)
+    side_y = jnp.zeros((NX_LOC + 2, WINDOW, NZ), bf16)
+    wext[0] = side_x
+    wext[NX_LOC + 1] = side_x
+    wext[:, 0] = side_y
+    wext[:, NY_LOC + 1] = side_y
+
+    def turned(plane):
+        return jnp.swapaxes(plane.astype(f32), 0, 1).astype(bf16)
+
+    loads[0].wait()
+    loads[1].wait()
+    wext[1, inner_y] = turned(fac_ends[0, pl.ds(start, WINDOW)])
+    wext[NX_LOC, inner_y] = turned(fac_ends[1, pl.ds(start, WINDOW)])
+    pl.semaphore_wait(barrier, count)
     moves = (
-        (wext.at[NX_LOC, inner_y], wext.at[0, inner_y], right),
-        (wext.at[1, inner_y], wext.at[NX_LOC + 1, inner_y], left),
-        (wext.at[inner_x, NY_LOC], wext.at[inner_x, 0], up),
-        (wext.at[inner_x, 1], wext.at[inner_x, NY_LOC + 1], down),
+        (wext.at[NX_LOC, inner_y], xhalo.at[0], right),
+        (wext.at[1, inner_y], xhalo.at[1], left),
+        (wext.at[inner_x, NY_LOC], yhalo.at[0], up),
+        (wext.at[inner_x, 1], yhalo.at[1], down),
     )
-    copies = []
-    for at, (source, target, who) in enumerate(moves):
-        copy = pltpu.make_async_remote_copy(source, target, hs_sem.at[at], hr_sem.at[at], device_id=who, device_id_type=MESH)
-        copy.start()
-        copies.append(copy)
+    copies = [pltpu.make_async_remote_copy(source, target, hs_sem.at[at], hr_sem.at[at], device_id=who, device_id_type=MESH)
+              for at, (source, target, who) in enumerate(moves)]
+    copies[0].start()
+    copies[1].start()
+    loads[2].wait()
+
+    def turn(x, carry):
+        wext[x + 2, inner_y] = turned(fac_mid[pl.ds(start, WINDOW), x])
+        return carry
+
+    lax.fori_loop(0, NX_LOC - 2, turn, 0)
+    copies[2].start()
+    copies[3].start()
 
     def gram_plane(x, total):
         part = jnp.zeros((WINDOW, WINDOW), f32)
@@ -153,11 +173,11 @@
     gram_sum.send(0, fold(gram_local))
     w_write = pltpu.make_async_copy(wext.at[inner_x, inner_y], w_hbm, out_sem.at[0])
     w_write.start()
-    for load in loads[1:]:
+    for load in loads[3:]:
         load.wait()
 
     def turn_io(x, carry):
-        io_t[x] = jnp.swapaxes(io[:, x].astype(f32), 0, 1).astype(bf16)
+        io_t[x] = turned(io[:, x])
         return carry
 
     lax.fori_loop(0, NX_LOC, turn_io, 0)
@@ -165,60 +185,56 @@
 
     lane = lax.broadcasted_iota(jnp.int32, (WINDOW, NZ), 1)
 
-    def line(x, y):
-        w16 = wext[x + 1, y + 1]
-        w = w16.astype(f32)
-        beside = wext[x + 2, y + 1].astype(f32) + wext[x, y + 1].astype(f32)
-        beside = beside + wext[x + 1, y + 2].astype(f32) + wext[x + 1, y].astype(f32)
-        beside = beside + jnp.where(lane == NZ - 1, 0.0, pltpu.roll(w, NZ - 1, 1))
-        beside = beside + jnp.where(lane == 0, 0.0, pltpu.roll(w, 1, 1))
-        image = beside - (6.0 + diag_ref[x, y:y + 1, :]) * w
-        parts = jnp.concatenate(pieces(image, 3), axis=0)
-        awbuf[x, y] = parts
-        return bdot(jnp.concatenate([parts, io_t[x, y]], axis=0), w16, ((1,), (1,)))
-
-    def lines(ys):
-        def body(x, total):
-            part = jnp.zeros((112, WINDOW), f32)
-            for y in ys:
-                part = part + line(x, y)
-            return total + part
-        return body
-
-    total = lax.fori_loop(1, NX_LOC - 1, lines(range(1, NY_LOC - 1)), jnp.zeros((112, WINDOW), f32))
+    def inside_plane(x, total):
+        part = jnp.zeros((112, WINDOW), f32)
+        for y in range(NY_LOC):
+            w16 = wext[x + 1, y + 1]
+            w = w16.astype(f32)
+            beside = wext[x + 2, y + 1].astype(f32) + wext[x, y + 1].astype(f32)
+            beside = beside + wext[x + 1, y + 2].astype(f32) + wext[x + 1, y].astype(f32)
+            beside = beside + jnp.where(lane == NZ - 1, 0.0, pltpu.roll(w, NZ - 1, 1))
+            beside = beside + jnp.where(lane == 0, 0.0, pltpu.roll(w, 1, 1))
+            image = beside - (6.0 + diag_ref[x, y:y + 1, :]) * w
+            parts = jnp.concatenate(pieces(image, 3), axis=0)
+            awbuf[x, y] = parts
+            part = part + bdot(jnp.concatenate([parts, io_t[x, y]], axis=0), w16, ((1,), (1,)))
+        return total + part
+
+    total = lax.fori_loop(0, NX_LOC, inside_plane, jnp.zeros((112, WINDOW), f32))
+    cross = total[0:32] + (total[32:64] + total[64:96])
     for copy in copies:
         copy.wait()
-    w_write.wait()
-
-    @pl.when(gx == 0)
-    def _():
-        wext[0] = jnp.zeros_like(wext[0])
-
-    @pl.when(gx == 31)
-    def _():
-        wext[NX_LOC + 1] = jnp.zeros_like(wext[0])
-
-    @pl.when(gz == 0)
-    def _():
-        wext[:, 0] = jnp.zeros_like(wext[:, 0])
-
-    @pl.when(gz == 7)
-    def _():
-        wext[:, NY_LOC + 1] = jnp.zeros_like(wext[:, 0])
-
-    def edge(step, total):
-        return lines((0, NY_LOC - 1))(2 * step + 2, lines((0, NY_LOC - 1))(2 * step + 1, total))
-
-    total = lax.fori_loop(0, (NX_LOC - 2) // 2, edge, total)
-    total = lax.fori_loop(0, 2, lambda at, t: lines(range(NY_LOC))(at * (NX_LOC - 1), t), total)
-    total = total * (1.0 / CELLS)
-    cross = total[0:32] + (total[32:64] + total[64:96])
-    io_sum = jnp.concatenate([total[96:104], total[104:112], jnp.zeros((8, 64), f32)], axis=1)
-    cross_sum.send(0, jnp.concatenate([fold(cross), io_sum], axis=0))
+
+    for edge, halo in ((gx == 0, xhalo.at[0]), (gx == 31, xhalo.at[1]), (gz == 0, yhalo.at[0]), (gz == 7, yhalo.at[1])):
+        @pl.when(edge)
+        def _(halo=halo):
+            halo[...] = jnp.zeros_like(halo)
+
+    for y in range(NY_LOC):
+        cross = cross + bdot(xhalo[0, y], wext[1, y + 1], ((1,), (1,)))
+        cross = cross + bdot(xhalo[1, y], wext[NX_LOC, y + 1], ((1,), (1,)))
+    for x in range(NX_LOC):
+        cross = cross + bdot(yhalo[0, x], wext[x + 1, 1], ((1,), (1,)))
+        cross = cross + bdot(yhalo[1, x], wext[x + 1, NY_LOC], ((1,), (1,)))
+    io_part = total[96:112]
+    io_fold = jnp.concatenate([io_part[4 * q:4 * q + 4] for q in range(4)], axis=1)
+    cross_sum.send(0, jnp.concatenate([fold(cross), io_fold], axis=0) * (1.0 / CELLS))
+
+    def add_layer(x, y, halo):
+        parts = awbuf[x, y].astype(f32)
+        image = parts[0:32] + (parts[32:64] + parts[64:96]) + halo.astype(f32)
+        awbuf[x, y] = jnp.concatenate(pieces(image, 3), axis=0)
+
+    for y in range(NY_LOC):
+        add_layer(0, y, xhalo[0, y])
+        add_layer(last, y, xhalo[1, y])
+    for x in range(NX_LOC):
+        add_layer(x, 0, yhalo[0, x])
+        add_layer(x, NY_LOC - 1, yhalo[1, x])
+    cross_sum.send(1, cross_sum.receive(0))
     aw_write = pltpu.make_async_copy(awbuf, aw_hbm, out_sem.at[1])
     aw_write.start()
     gram_sum.send(2, gram_sum.receive(1))
-    cross_sum.send(1, cross_sum.receive(0))
     cross_sum.send(2, cross_sum.receive(1))
     gram = unfold(gram_sum.receive(2))
     ident = eye(WINDOW)
@@ -230,13 +246,14 @@
     transform = dot(inverse_second, inverse_first)
     received = cross_sum.receive(2)
     cross = unfold(received[0:8])
-    io_rows = jnp.concatenate([received[8:16, 0:32], received[8:16, 32:64]], axis=0)
+    io_rows = jnp.concatenate([received[8:12, 32 * q:32 * q + 32] for q in range(4)], axis=0)
     raw = dot(dot(transform, cross), transform, ((1,), (1,)))
     io_basis = dot(transform, io_rows, ((1,), (1,)))
     small_ref[0:32] = jnp.concatenate([raw, transform, io_basis, jnp.zeros((WINDOW, 48), f32)], axis=1)
     small_ref[32:64] = jnp.concatenate([gram, jnp.zeros((WINDOW, 96), f32)], axis=1)
     gram_sum.finish()
     cross_sum.finish()
+    w_write.wait()
     aw_write.wait()
 
 
@@ -251,15 +268,16 @@
         in_specs=[pl.BlockSpec(memory_space=pltpu.SMEM), anywhere, anywhere, anywhere, anywhere],
         out_specs=(vmem, anywhere, anywhere),
         scratch_shapes=[
-            pltpu.VMEM((64, NX_LOC, NY_LOC, NZ), bf16),
+            pltpu.VMEM((2, 64, NY_LOC, NZ), bf16), pltpu.VMEM((64, NX_LOC - 2, NY_LOC, NZ), bf16),
             pltpu.VMEM((NX_LOC, NY_LOC, NZ), f32),
             pltpu.VMEM((2 * CONTROLS, NX_LOC, NY_LOC, NZ), bf16),
             pltpu.VMEM((NX_LOC + 2, NY_LOC + 2, WINDOW, NZ), bf16),
+            pltpu.VMEM((2, NY_LOC, WINDOW, NZ), bf16), pltpu.VMEM((2, NX_LOC, WINDOW, NZ), bf16),
             pltpu.VMEM((NX_LOC, NY_LOC, 2 * CONTROLS, NZ), bf16),
             pltpu.VMEM((NX_LOC, NY_LOC, 96, NZ), bf16),
             pltpu.VMEM((2, 8, 128), f32), pltpu.VMEM((16, 8, 128), f32), pltpu.VMEM((8, 8, 128), f32),
-            pltpu.VMEM((2, 16, 128), f32), pltpu.VMEM((16, 16, 128), f32), pltpu.VMEM((8, 16, 128), f32),
-            dma((4,)), dma((4,)), dma((4,)), dma((3,)), dma((3,)), dma((3,)), dma((3,)), dma((2,)),
+            pltpu.VMEM((2, 12, 128), f32), pltpu.VMEM((16, 12, 128), f32), pltpu.VMEM((8, 12, 128), f32),
+            dma((6,)), dma((4,)), dma((4,)), dma((3,)), dma((3,)), dma((3,)), dma((3,)), dma((2,)),
         ],
         compiler_params=pltpu.CompilerParams(collective_id=0, has_side_effects=True, vmem_limit_bytes=60 << 20),
         name="stats_all_reduce",
@@ -316,30 +334,31 @@
     drive_t, sense_t = drive.T, sense.T
     hd = dot3(inv_n, drive)
     hd_t = hd.T
+    sense_h = dot3(sense_t, inv_n)
+    sense_hd = dot3(sense_t, hd)
     chain = None
     for iteration in range(KLEIN):
         if chain is None:
             einv_t = -inv_n
-            rows = sense_t
+            chain = -sense_h
         else:
             q_t = 2.0 * dot3(dot3(drive_t, chain, ((1,), (1,))), chain)
             hq_t = dot3(q_t, inv_n)
+            q_hd = dot3(q_t, hd)
             small = eye(CONTROLS) + dot3(hd_t, q_t, ((1,), (1,)))
             normal = dot3(small, small, ((1,), (1,)))
             table = jnp.concatenate([normal, dot3(small, hq_t), jnp.zeros((CONTROLS, 88), f32)], axis=1)
             solved = sweep(table, CONTROLS, True)[:, CONTROLS:CONTROLS + WINDOW]
             einv_t = dot3(hd, solved) - inv_n
-            rows = jnp.concatenate([sense_t, q_t], axis=0)
+            chain = dot3(jnp.concatenate([sense_hd, q_hd], axis=0), solved) - jnp.concatenate([sense_h, hq_t], axis=0)
         cayley_t = ident + 2.0 * einv_t
-        chain = dot3(rows, einv_t)
         for doubling in range(SMITH):
             chain = jnp.concatenate([chain, dot3(chain, cayley_t)], axis=0)
             if doubling < SMITH - 1:
                 cayley_t = dot3(cayley_t, cayley_t)
     riccati = 2.0 * dot3(chain, chain, ((0,), (0,)))
-    rotate = dot(riccati, transform)
-    remain = dot(dot(riccati, projected), transform)
-    return rotate, remain, riccati, gram
+    both = dot(riccati, jnp.concatenate([transform, dot(projected, transform)], axis=1))
+    return both[:, :32], both[:, 32:], riccati, gram
 
 
 def output_kernel(small_ref, w_hbm, aw_hbm, rot_hbm, res_hbm, ric_ref, gram_ref,

time: 44.5 us -> 43.4 us (0.975); the launches traced: 43.8 us -> 43.2 us
  Pallas kernels: 42.5 us -> 41.9 us
    pallas_call x1, Pallas kernels: 29.8 us -> 29.4 us  [stats(): pl.pallas_call(stats_kernel, out_shape=(jax.ShapeDtypeStruct((64, 128), f...]
where the time goes in v3:
time: 43.4 us; the launch traced here: 43.2 us
  Pallas kernels  41.9 us (97%)
  between operations  1.28 us (3%)
    pallas_call x1, Pallas kernels, stats(): pl.pallas_call(stats_kernel, out_shape=(jax.ShapeDtypeStruct((64, 128), f...  29.4 us
    pallas_call x1, Pallas kernels, outputs(): pl.pallas_call(output_kernel, out_shape=(jax.ShapeDtypeStruct(field, bf16...  12.6 us

profile of v3, /device:TPU:1, one launch (start us, length us, event | category | flops | bytes accessed | tf_op | source)
XLA Modules:
  0.0 43.2 jit_solution(1796021004370118179)
XLA Ops:
  1.3 29.4 %stats_all_reduce.1 = (f32[64,128]{1,0:T(8,128)}, bf16[8,16,32,256]{3,2,1,0:T(8,128)(2,1)}, bf16[8,16,96,256]{3,2,1,0:T(8,128)(2,1)}) custom-call(s32[1]{0:T(128)S(6)} %copy.9.off_ref, bf16[64,8,16,256]{3,2,1,0:T(8,128)(2,1)} %fac_hbm.1, f32[8,16,256]{2,1,0:T(8,128)} %diag_hbm.1, bf16[8,8,16,256]{3,2,1,0:T(8,128)(2,1)} %act_hbm.1, ...), custom_call_target="tpu_custom_call" | custom-call | tf_op jit(solution)/shard_map/stats_all_reduce/pallas_call | solution.py:263
  30.6 12.6 %algebra_outputs.1 = (bf16[32,8,16,256]{3,2,1,0:T(8,128)(2,1)}, bf16[32,8,16,256]{3,2,1,0:T(8,128)(2,1)}, f32[32,32]{1,0:T(8,128)}, f32[32,32]{1,0:T(8,128)}) custom-call(f32[64,128]{1,0:T(8,128)} %get-tuple-element.7.small_ref, bf16[8,16,32,256]{3,2,1,0:T(8,128)(2,1)} %get-tuple-element.8.w_hbm, bf16[8,16,96,256]{3,2,1,0:T(8,128)(2,1)} %get-tuple-element.9.aw_hbm), custom_call_target="tpu_custom_call" | custom-call | tf_op jit(solution)/shard_map/algebra_outputs/pallas_call | solution.py:402

commit v4 on v3

--- a/solution.py
+++ b/solution.py
@@ -187,13 +187,15 @@
 
     def inside_plane(x, total):
         part = jnp.zeros((112, WINDOW), f32)
+        rows = [wext[x + 1, 0].astype(f32), wext[x + 1, 1].astype(f32)]
         for y in range(NY_LOC):
+            rows.append(wext[x + 1, y + 2].astype(f32))
             w16 = wext[x + 1, y + 1]
-            w = w16.astype(f32)
+            w = rows[y + 1]
             beside = wext[x + 2, y + 1].astype(f32) + wext[x, y + 1].astype(f32)
-            beside = beside + wext[x + 1, y + 2].astype(f32) + wext[x + 1, y].astype(f32)
-            beside = beside + jnp.where(lane == NZ - 1, 0.0, pltpu.roll(w, NZ - 1, 1))
-            beside = beside + jnp.where(lane == 0, 0.0, pltpu.roll(w, 1, 1))
+            beside = beside + rows[y + 2] + rows[y]
+            beside = beside + jnp.where(lane == NZ - 1, 0.0, pltpu.roll(w16, NZ - 1, 1).astype(f32))
+            beside = beside + jnp.where(lane == 0, 0.0, pltpu.roll(w16, 1, 1).astype(f32))
             image = beside - (6.0 + diag_ref[x, y:y + 1, :]) * w
             parts = jnp.concatenate(pieces(image, 3), axis=0)
             awbuf[x, y] = parts
@@ -374,17 +376,16 @@
     zero = jnp.zeros((WINDOW, WINDOW), bf16)
     cat = lambda *blocks: jnp.concatenate(blocks, axis=1)
     coef[...] = jnp.concatenate([
-        cat(r0, zero, zero, zero), cat(m0, r0, r0, r0),
-        cat(r1, zero, zero, zero), cat(m1, r1, r1, zero),
-        cat(r2, zero, zero, zero), cat(m2, r2, zero, zero)], axis=0)
+        cat(r0, zero, zero, zero, r2, zero), cat(m0, r0, r0, r0, m2, r2),
+        cat(r1, zero, zero, zero, zero, zero), cat(m1, r1, r1, zero, zero, zero)], axis=0)
     for load in loads:
         load.wait()
 
     def plane(x, carry):
         for y in range(NY_LOC):
-            data = jnp.concatenate([wbuf[x, y], awbuf[x, y]], axis=0)
-            out = bdot(coef[...], data)
-            tmp[y] = out[0:64] + (out[64:128] + out[128:192])
+            w, parts = wbuf[x, y], awbuf[x, y]
+            out = bdot(coef[...], jnp.concatenate([w, parts, w, parts[0:32]], axis=0))
+            tmp[y] = out[0:64] + out[64:128]
         rot[x] = jnp.swapaxes(tmp[:, 0:32, :], 0, 1).astype(bf16)
         res[x] = jnp.swapaxes(tmp[:, 32:64, :], 0, 1).astype(bf16)
         pltpu.make_async_copy(rot.at[x], rot_hbm.at[:, x], out_sem.at[0]).start()
@@ -408,7 +409,7 @@
         scratch_shapes=[
             pltpu.VMEM((NX_LOC, NY_LOC, WINDOW, NZ), bf16), pltpu.VMEM((NX_LOC, NY_LOC, 96, NZ), bf16),
             pltpu.VMEM((NX_LOC, WINDOW, NY_LOC, NZ), bf16), pltpu.VMEM((NX_LOC, WINDOW, NY_LOC, NZ), bf16),
-            pltpu.VMEM((192, 128), bf16), pltpu.VMEM((NY_LOC, 64, NZ), f32),
+            pltpu.VMEM((128, 192), bf16), pltpu.VMEM((NY_LOC, 64, NZ), f32),
             pltpu.SemaphoreType.DMA((2,)), pltpu.SemaphoreType.DMA((2,)),
         ],
         compiler_params=pltpu.CompilerParams(vmem_limit_bytes=60 << 20),

time: 43.4 us -> 42 us (0.968)
  Pallas kernels: 41.9 us -> 40.5 us
    pallas_call x1, Pallas kernels: 12.6 us -> 11.6 us  [outputs(): pl.pallas_call(output_kernel, out_shape=(jax.ShapeDtypeStruct(field, bf16...]
    pallas_call x1, Pallas kernels: 29.4 us -> 28.9 us  [stats(): pl.pallas_call(stats_kernel, out_shape=(jax.ShapeDtypeStruct((64, 128), f...]
where the time goes in v4:
time: 42 us; the launch traced here: 41.8 us
  Pallas kernels  40.5 us (96%)
  between operations  1.28 us (3%)
    pallas_call x1, Pallas kernels, stats(): pl.pallas_call(stats_kernel, out_shape=(jax.ShapeDtypeStruct((64, 128), f...  28.9 us
    pallas_call x1, Pallas kernels, outputs(): pl.pallas_call(output_kernel, out_shape=(jax.ShapeDtypeStruct(field, bf16...  11.6 us

profile of v4, /device:TPU:1, one launch (start us, length us, event | category | flops | bytes accessed | tf_op | source)
XLA Modules:
  0.0 41.8 jit_solution(5052516907717930249)
XLA Ops:
  1.3 28.9 %stats_all_reduce.1 = (f32[64,128]{1,0:T(8,128)}, bf16[8,16,32,256]{3,2,1,0:T(8,128)(2,1)}, bf16[8,16,96,256]{3,2,1,0:T(8,128)(2,1)}) custom-call(s32[1]{0:T(128)S(6)} %copy.9.off_ref, bf16[64,8,16,256]{3,2,1,0:T(8,128)(2,1)} %fac_hbm.1, f32[8,16,256]{2,1,0:T(8,128)} %diag_hbm.1, bf16[8,8,16,256]{3,2,1,0:T(8,128)(2,1)} %act_hbm.1, ...), custom_call_target="tpu_custom_call" | custom-call | tf_op jit(solution)/shard_map/stats_all_reduce/pallas_call | solution.py:265
  30.2 11.6 %algebra_outputs.1 = (bf16[32,8,16,256]{3,2,1,0:T(8,128)(2,1)}, bf16[32,8,16,256]{3,2,1,0:T(8,128)(2,1)}, f32[32,32]{1,0:T(8,128)}, f32[32,32]{1,0:T(8,128)}) custom-call(f32[64,128]{1,0:T(8,128)} %get-tuple-element.7.small_ref, bf16[8,16,32,256]{3,2,1,0:T(8,128)(2,1)} %get-tuple-element.8.w_hbm, bf16[8,16,96,256]{3,2,1,0:T(8,128)(2,1)} %get-tuple-element.9.aw_hbm), custom_call_target="tpu_custom_call" | custom-call | tf_op jit(solution)/shard_map/algebra_outputs/pallas_call | solution.py:403

commit v5 on v4

--- a/solution.py
+++ b/solution.py
@@ -139,6 +139,13 @@
     loads[1].wait()
     wext[1, inner_y] = turned(fac_ends[0, pl.ds(start, WINDOW)])
     wext[NX_LOC, inner_y] = turned(fac_ends[1, pl.ds(start, WINDOW)])
+    loads[2].wait()
+
+    def turn(x, carry):
+        wext[x + 2, inner_y] = turned(fac_mid[pl.ds(start, WINDOW), x])
+        return carry
+
+    lax.fori_loop(0, NX_LOC - 2, turn, 0)
     pl.semaphore_wait(barrier, count)
     moves = (
         (wext.at[NX_LOC, inner_y], xhalo.at[0], right),
@@ -148,17 +155,8 @@
     )
     copies = [pltpu.make_async_remote_copy(source, target, hs_sem.at[at], hr_sem.at[at], device_id=who, device_id_type=MESH)
               for at, (source, target, who) in enumerate(moves)]
-    copies[0].start()
-    copies[1].start()
-    loads[2].wait()
-
-    def turn(x, carry):
-        wext[x + 2, inner_y] = turned(fac_mid[pl.ds(start, WINDOW), x])
-        return carry
-
-    lax.fori_loop(0, NX_LOC - 2, turn, 0)
-    copies[2].start()
-    copies[3].start()
+    for copy in copies:
+        copy.start()
 
     def gram_plane(x, total):
         part = jnp.zeros((WINDOW, WINDOW), f32)
@@ -358,7 +356,8 @@
             chain = jnp.concatenate([chain, dot3(chain, cayley_t)], axis=0)
             if doubling < SMITH - 1:
                 cayley_t = dot3(cayley_t, cayley_t)
-    riccati = 2.0 * dot3(chain, chain, ((0,), (0,)))
+    halves = [chain[:128].T, chain[128:].T]
+    riccati = 2.0 * (dot3(halves[0], halves[0], ((1,), (1,))) + dot3(halves[1], halves[1], ((1,), (1,))))
     both = dot(riccati, jnp.concatenate([transform, dot(projected, transform)], axis=1))
     return both[:, :32], both[:, 32:], riccati, gram
 

time: 42 us -> 41.8 us (level)
  no operation moved by 1% of the time
where the time goes in v5:
time: 41.8 us; the launch traced here: 41.7 us
  Pallas kernels  40.4 us (97%)
  between operations  1.28 us (3%)
    pallas_call x1, Pallas kernels, stats(): pl.pallas_call(stats_kernel, out_shape=(jax.ShapeDtypeStruct((64, 128), f...  28.8 us
    pallas_call x1, Pallas kernels, outputs(): pl.pallas_call(output_kernel, out_shape=(jax.ShapeDtypeStruct(field, bf16...  11.5 us

profile of v5, /device:TPU:1, one launch (start us, length us, event | category | flops | bytes accessed | tf_op | source)
XLA Modules:
  0.0 41.7 jit_solution(17153131034896091609)
XLA Ops:
  1.3 28.8 %stats_all_reduce.1 = (f32[64,128]{1,0:T(8,128)}, bf16[8,16,32,256]{3,2,1,0:T(8,128)(2,1)}, bf16[8,16,96,256]{3,2,1,0:T(8,128)(2,1)}) custom-call(s32[1]{0:T(128)S(6)} %copy.9.off_ref, bf16[64,8,16,256]{3,2,1,0:T(8,128)(2,1)} %fac_hbm.1, f32[8,16,256]{2,1,0:T(8,128)} %diag_hbm.1, bf16[8,8,16,256]{3,2,1,0:T(8,128)(2,1)} %act_hbm.1, ...), custom_call_target="tpu_custom_call" | custom-call | tf_op jit(solution)/shard_map/stats_all_reduce/pallas_call | solution.py:263
  30.1 11.5 %algebra_outputs.1 = (bf16[32,8,16,256]{3,2,1,0:T(8,128)(2,1)}, bf16[32,8,16,256]{3,2,1,0:T(8,128)(2,1)}, f32[32,32]{1,0:T(8,128)}, f32[32,32]{1,0:T(8,128)}) custom-call(f32[64,128]{1,0:T(8,128)} %get-tuple-element.7.small_ref, bf16[8,16,32,256]{3,2,1,0:T(8,128)(2,1)} %get-tuple-element.8.w_hbm, bf16[8,16,96,256]{3,2,1,0:T(8,128)(2,1)} %get-tuple-element.9.aw_hbm), custom_call_target="tpu_custom_call" | custom-call | tf_op jit(solution)/shard_map/algebra_outputs/pallas_call | solution.py:402

commit v6 on v5

--- a/solution.py
+++ b/solution.py
@@ -133,7 +133,7 @@
     wext[:, NY_LOC + 1] = side_y
 
     def turned(plane):
-        return jnp.swapaxes(plane.astype(f32), 0, 1).astype(bf16)
+        return jnp.swapaxes(plane, 0, 1)
 
     loads[0].wait()
     loads[1].wait()
@@ -220,6 +220,8 @@
     io_fold = jnp.concatenate([io_part[4 * q:4 * q + 4] for q in range(4)], axis=1)
     cross_sum.send(0, jnp.concatenate([fold(cross), io_fold], axis=0) * (1.0 / CELLS))
 
+    cross_sum.send(1, cross_sum.receive(0))
+    gram_sum.send(2, gram_sum.receive(1))
     def add_layer(x, y, halo):
         parts = awbuf[x, y].astype(f32)
         image = parts[0:32] + (parts[32:64] + parts[64:96]) + halo.astype(f32)
@@ -231,10 +233,8 @@
     for x in range(NX_LOC):
         add_layer(x, 0, yhalo[0, x])
         add_layer(x, NY_LOC - 1, yhalo[1, x])
-    cross_sum.send(1, cross_sum.receive(0))
     aw_write = pltpu.make_async_copy(awbuf, aw_hbm, out_sem.at[1])
     aw_write.start()
-    gram_sum.send(2, gram_sum.receive(1))
     cross_sum.send(2, cross_sum.receive(1))
     gram = unfold(gram_sum.receive(2))
     ident = eye(WINDOW)
@@ -384,9 +384,9 @@
         for y in range(NY_LOC):
             w, parts = wbuf[x, y], awbuf[x, y]
             out = bdot(coef[...], jnp.concatenate([w, parts, w, parts[0:32]], axis=0))
-            tmp[y] = out[0:64] + out[64:128]
-        rot[x] = jnp.swapaxes(tmp[:, 0:32, :], 0, 1).astype(bf16)
-        res[x] = jnp.swapaxes(tmp[:, 32:64, :], 0, 1).astype(bf16)
+            tmp[y] = (out[0:64] + out[64:128]).astype(bf16)
+        rot[x] = jnp.swapaxes(tmp[:, 0:32, :], 0, 1)
+        res[x] = jnp.swapaxes(tmp[:, 32:64, :], 0, 1)
         pltpu.make_async_copy(rot.at[x], rot_hbm.at[:, x], out_sem.at[0]).start()
         pltpu.make_async_copy(res.at[x], res_hbm.at[:, x], out_sem.at[1]).start()
         return carry
@@ -408,7 +408,7 @@
         scratch_shapes=[
             pltpu.VMEM((NX_LOC, NY_LOC, WINDOW, NZ), bf16), pltpu.VMEM((NX_LOC, NY_LOC, 96, NZ), bf16),
             pltpu.VMEM((NX_LOC, WINDOW, NY_LOC, NZ), bf16), pltpu.VMEM((NX_LOC, WINDOW, NY_LOC, NZ), bf16),
-            pltpu.VMEM((128, 192), bf16), pltpu.VMEM((NY_LOC, 64, NZ), f32),
+            pltpu.VMEM((128, 192), bf16), pltpu.VMEM((NY_LOC, 64, NZ), bf16),
             pltpu.SemaphoreType.DMA((2,)), pltpu.SemaphoreType.DMA((2,)),
         ],
         compiler_params=pltpu.CompilerParams(vmem_limit_bytes=60 << 20),

time: 41.8 us -> 41.3 us (0.988)
  Pallas kernels: 40.4 us -> 39.7 us
    pallas_call x1, Pallas kernels: 28.8 us -> 28.4 us  [stats(): pl.pallas_call(stats_kernel, out_shape=(jax.ShapeDtypeStruct((64, 128), f...]
where the time goes in v6:
time: 41.3 us; the launch traced here: 41 us
  Pallas kernels  39.7 us (96%)
  between operations  1.28 us (3%)
    pallas_call x1, Pallas kernels, stats(): pl.pallas_call(stats_kernel, out_shape=(jax.ShapeDtypeStruct((64, 128), f...  28.4 us
    pallas_call x1, Pallas kernels, outputs(): pl.pallas_call(output_kernel, out_shape=(jax.ShapeDtypeStruct(field, bf16...  11.3 us

profile of v6, /device:TPU:1, one launch (start us, length us, event | category | flops | bytes accessed | tf_op | source)
XLA Modules:
  0.0 41.0 jit_solution(16624669549174607027)
XLA Ops:
  1.3 28.4 %stats_all_reduce.1 = (f32[64,128]{1,0:T(8,128)}, bf16[8,16,32,256]{3,2,1,0:T(8,128)(2,1)}, bf16[8,16,96,256]{3,2,1,0:T(8,128)(2,1)}) custom-call(s32[1]{0:T(128)S(6)} %copy.9.off_ref, bf16[64,8,16,256]{3,2,1,0:T(8,128)(2,1)} %fac_hbm.1, f32[8,16,256]{2,1,0:T(8,128)} %diag_hbm.1, bf16[8,8,16,256]{3,2,1,0:T(8,128)(2,1)} %act_hbm.1, ...), custom_call_target="tpu_custom_call" | custom-call | tf_op jit(solution)/shard_map/stats_all_reduce/pallas_call | solution.py:263
  29.6 11.3 %algebra_outputs.1 = (bf16[32,8,16,256]{3,2,1,0:T(8,128)(2,1)}, bf16[32,8,16,256]{3,2,1,0:T(8,128)(2,1)}, f32[32,32]{1,0:T(8,128)}, f32[32,32]{1,0:T(8,128)}) custom-call(f32[64,128]{1,0:T(8,128)} %get-tuple-element.7.small_ref, bf16[8,16,32,256]{3,2,1,0:T(8,128)(2,1)} %get-tuple-element.8.w_hbm, bf16[8,16,96,256]{3,2,1,0:T(8,128)(2,1)} %get-tuple-element.9.aw_hbm), custom_call_target="tpu_custom_call" | custom-call | tf_op jit(solution)/shard_map/algebra_outputs/pallas_call | solution.py:402

commit v7 on v6

--- a/solution.py
+++ b/solution.py
@@ -98,14 +98,15 @@
 
 
 def stats_kernel(off_ref, fac_hbm, diag_hbm, act_hbm, sen_hbm, small_ref, w_hbm, aw_hbm,
-                 fac_ends, fac_mid, diag_ref, io, wext, xhalo, yhalo, io_t, awbuf, g0, g1, g2, s0, s1, s2,
+                 fac, diag_ref, io, wext, xhalo, yhalo, io_t, awbuf, g0, g1, g2, s0, s1, s2,
                  in_sem, hs_sem, hr_sem, gs_sem, gr_sem, ss_sem, sr_sem, out_sem):
     gx = lax.axis_index("gx")
     gz = lax.axis_index("gy")
     last = NX_LOC - 1
-    loads = [pltpu.make_async_copy(fac_hbm.at[:, 0], fac_ends.at[0], in_sem.at[0]),
-             pltpu.make_async_copy(fac_hbm.at[:, last], fac_ends.at[1], in_sem.at[1]),
-             pltpu.make_async_copy(fac_hbm.at[:, pl.ds(1, NX_LOC - 2)], fac_mid, in_sem.at[2]),
+    third = 24
+    loads = [pltpu.make_async_copy(fac_hbm.at[pl.ds(0, third)], fac.at[pl.ds(0, third)], in_sem.at[0]),
+             pltpu.make_async_copy(fac_hbm.at[pl.ds(third, third)], fac.at[pl.ds(third, third)], in_sem.at[1]),
+             pltpu.make_async_copy(fac_hbm.at[pl.ds(2 * third, 64 - 2 * third)], fac.at[pl.ds(2 * third, 64 - 2 * third)], in_sem.at[2]),
              pltpu.make_async_copy(act_hbm, io.at[pl.ds(0, CONTROLS)], in_sem.at[3]),
              pltpu.make_async_copy(sen_hbm, io.at[pl.ds(CONTROLS, CONTROLS)], in_sem.at[4]),
              pltpu.make_async_copy(diag_hbm, diag_ref, in_sem.at[5])]
@@ -135,17 +136,14 @@
     def turned(plane):
         return jnp.swapaxes(plane, 0, 1)
 
-    loads[0].wait()
-    loads[1].wait()
-    wext[1, inner_y] = turned(fac_ends[0, pl.ds(start, WINDOW)])
-    wext[NX_LOC, inner_y] = turned(fac_ends[1, pl.ds(start, WINDOW)])
-    loads[2].wait()
+    for load in loads[:3]:
+        load.wait()
 
     def turn(x, carry):
-        wext[x + 2, inner_y] = turned(fac_mid[pl.ds(start, WINDOW), x])
+        wext[x + 1, inner_y] = turned(fac[pl.ds(start, WINDOW), x])
         return carry
 
-    lax.fori_loop(0, NX_LOC - 2, turn, 0)
+    lax.fori_loop(0, NX_LOC, turn, 0)
     pl.semaphore_wait(barrier, count)
     moves = (
         (wext.at[NX_LOC, inner_y], xhalo.at[0], right),
@@ -268,7 +266,7 @@
         in_specs=[pl.BlockSpec(memory_space=pltpu.SMEM), anywhere, anywhere, anywhere, anywhere],
         out_specs=(vmem, anywhere, anywhere),
         scratch_shapes=[
-            pltpu.VMEM((2, 64, NY_LOC, NZ), bf16), pltpu.VMEM((64, NX_LOC - 2, NY_LOC, NZ), bf16),
+            pltpu.VMEM((64, NX_LOC, NY_LOC, NZ), bf16),
             pltpu.VMEM((NX_LOC, NY_LOC, NZ), f32),
             pltpu.VMEM((2 * CONTROLS, NX_LOC, NY_LOC, NZ), bf16),
             pltpu.VMEM((NX_LOC + 2, NY_LOC + 2, WINDOW, NZ), bf16),

time: 41.3 us -> 41.5 us (level)
  no operation moved by 1% of the time
where the time goes in v7:
time: 41.5 us; the launch traced here: 41.1 us
  Pallas kernels  39.8 us (96%)
  between operations  1.28 us (3%)
    pallas_call x1, Pallas kernels, stats(): pl.pallas_call(stats_kernel, out_shape=(jax.ShapeDtypeStruct((64, 128), f...  28.5 us
    pallas_call x1, Pallas kernels, outputs(): pl.pallas_call(output_kernel, out_shape=(jax.ShapeDtypeStruct(field, bf16...  11.3 us

profile of v7, /device:TPU:1, one launch (start us, length us, event | category | flops | bytes accessed | tf_op | source)
XLA Modules:
  0.0 41.1 jit_solution(7398971590437030582)
XLA Ops:
  1.3 28.5 %stats_all_reduce.1 = (f32[64,128]{1,0:T(8,128)}, bf16[8,16,32,256]{3,2,1,0:T(8,128)(2,1)}, bf16[8,16,96,256]{3,2,1,0:T(8,128)(2,1)}) custom-call(s32[1]{0:T(128)S(6)} %copy.9.off_ref, bf16[64,8,16,256]{3,2,1,0:T(8,128)(2,1)} %fac_hbm.1, f32[8,16,256]{2,1,0:T(8,128)} %diag_hbm.1, bf16[8,8,16,256]{3,2,1,0:T(8,128)(2,1)} %act_hbm.1, ...), custom_call_target="tpu_custom_call" | custom-call | tf_op jit(solution)/shard_map/stats_all_reduce/pallas_call | solution.py:261
  29.7 11.3 %algebra_outputs.1 = (bf16[32,8,16,256]{3,2,1,0:T(8,128)(2,1)}, bf16[32,8,16,256]{3,2,1,0:T(8,128)(2,1)}, f32[32,32]{1,0:T(8,128)}, f32[32,32]{1,0:T(8,128)}) custom-call(f32[64,128]{1,0:T(8,128)} %get-tuple-element.7.small_ref, bf16[8,16,32,256]{3,2,1,0:T(8,128)(2,1)} %get-tuple-element.8.w_hbm, bf16[8,16,96,256]{3,2,1,0:T(8,128)(2,1)} %get-tuple-element.9.aw_hbm), custom_call_target="tpu_custom_call" | custom-call | tf_op jit(solution)/shard_map/algebra_outputs/pallas_call | solution.py:400

commit v8 on v6

--- a/solution.py
+++ b/solution.py
@@ -109,8 +109,6 @@
              pltpu.make_async_copy(act_hbm, io.at[pl.ds(0, CONTROLS)], in_sem.at[3]),
              pltpu.make_async_copy(sen_hbm, io.at[pl.ds(CONTROLS, CONTROLS)], in_sem.at[4]),
              pltpu.make_async_copy(diag_hbm, diag_ref, in_sem.at[5])]
-    for load in loads:
-        load.start()
     barrier = pltpu.get_barrier_semaphore()
     right, left = ((gx + 1) % 32, gz), ((gx + 31) % 32, gz)
     up, down = (gx, (gz + 1) % 8), (gx, (gz + 7) % 8)
@@ -122,6 +120,8 @@
     for target in (right, left):
         pl.semaphore_signal(barrier, inc=1, device_id=target, device_id_type=MESH)
         count += 1
+    for load in loads:
+        load.start()
     start = off_ref[0]
     inner_y = pl.ds(1, NY_LOC)
     inner_x = pl.ds(1, NX_LOC)

time: 41.3 us -> 41.5 us (level)
  no operation moved by 1% of the time
where the time goes in v8:
time: 41.5 us; the launch traced here: 41.3 us
  Pallas kernels  40 us (96%)
  between operations  1.28 us (3%)
    pallas_call x1, Pallas kernels, stats(): pl.pallas_call(stats_kernel, out_shape=(jax.ShapeDtypeStruct((64, 128), f...  28.7 us
    pallas_call x1, Pallas kernels, outputs(): pl.pallas_call(output_kernel, out_shape=(jax.ShapeDtypeStruct(field, bf16...  11.3 us

profile of v8, /device:TPU:1, one launch (start us, length us, event | category | flops | bytes accessed | tf_op | source)
XLA Modules:
  0.0 41.3 jit_solution(18299317520629896579)
XLA Ops:
  1.3 28.7 %stats_all_reduce.1 = (f32[64,128]{1,0:T(8,128)}, bf16[8,16,32,256]{3,2,1,0:T(8,128)(2,1)}, bf16[8,16,96,256]{3,2,1,0:T(8,128)(2,1)}) custom-call(s32[1]{0:T(128)S(6)} %copy.9.off_ref, bf16[64,8,16,256]{3,2,1,0:T(8,128)(2,1)} %fac_hbm.1, f32[8,16,256]{2,1,0:T(8,128)} %diag_hbm.1, bf16[8,8,16,256]{3,2,1,0:T(8,128)(2,1)} %act_hbm.1, ...), custom_call_target="tpu_custom_call" | custom-call | tf_op jit(solution)/shard_map/stats_all_reduce/pallas_call | solution.py:263
  30.0 11.3 %algebra_outputs.1 = (bf16[32,8,16,256]{3,2,1,0:T(8,128)(2,1)}, bf16[32,8,16,256]{3,2,1,0:T(8,128)(2,1)}, f32[32,32]{1,0:T(8,128)}, f32[32,32]{1,0:T(8,128)}) custom-call(f32[64,128]{1,0:T(8,128)} %get-tuple-element.7.small_ref, bf16[8,16,32,256]{3,2,1,0:T(8,128)(2,1)} %get-tuple-element.8.w_hbm, bf16[8,16,96,256]{3,2,1,0:T(8,128)(2,1)} %get-tuple-element.9.aw_hbm), custom_call_target="tpu_custom_call" | custom-call | tf_op jit(solution)/shard_map/algebra_outputs/pallas_call | solution.py:402
